TPU v7x, 32 devices: a whole 2x2x4 slice. The times are simulated.
32 devices in a mesh: dp: 16 (over z, y, core), mp: 2 (over x).
Axes of the slice: x: 2, y: 2, z: 4, core: 2. Of those that a mesh axis runs over, the one named last changes fastest.
Arguments:
- tokens: bfloat16 [32768, 768], P('dp'), may hold values from -6 to 6
- grad_out: bfloat16 [32768, 768], P('dp'), may hold values from -6 to 6
- head_perm: int32 [32, 12], P('dp', 'mp'), may hold values from 0 to 1
- block_mask: int32 [32, 12, 3], P('dp', 'mp'), may hold values 0 or 1
- w_qkv: bfloat16 [768, 3, 768], P('dp', None, 'mp'), may hold values from -0.3125 to 0.3125
- b_qv: bfloat16 [2, 768], P(None, ('mp', 'dp')), may hold values from -3 to 3
- w_out: bfloat16 [768, 768], P('mp', 'dp'), may hold values from -0.625 to 0.625
- b_out: bfloat16 [768], P('dp'), may hold values from -3 to 3
- gain_one: bfloat16 [768], P('dp'), may hold values from 0.25 to 1.75
- shift_one: bfloat16 [768], P('dp'), may hold values from -2 to 2
- w_up: bfloat16 [768, 3072], P('dp', 'mp'), may hold values from -0.21875 to 0.21875
- b_up: bfloat16 [3072], P(('mp', 'dp')), may hold values from -3 to 3
- w_down: bfloat16 [3072, 768], P('mp', 'dp'), may hold values from -0.15625 to 0.15625
- b_down: bfloat16 [768], P('dp'), may hold values from -2 to 2
- gain_two: bfloat16 [768], P('dp'), may hold values from 0.25 to 1.75
- shift_two: bfloat16 [768], P('dp'), may hold values from -2 to 2
Outputs:
- output: bfloat16 [32768, 768], P('dp')
- input_grad: float32 [32768, 768], P('dp')
- grad_w_qkv: float32 [768, 3, 768], P('dp', None, 'mp')
- grad_b_qv: float32 [2, 768], P(None, ('mp', 'dp'))
- grad_w_out: float32 [768, 768], P('mp', 'dp')
- grad_b_out: float32 [768], P('dp')
- grad_gain_one: float32 [768], P('dp')
- grad_shift_one: float32 [768], P('dp')
- grad_w_up: float32 [768, 3072], P('dp', 'mp')
- grad_b_up: float32 [3072], P(('mp', 'dp'))
- grad_w_down: float32 [3072, 768], P('mp', 'dp')
- grad_b_down: float32 [768], P('dp')
- grad_gain_two: float32 [768], P('dp')
- grad_shift_two: float32 [768], P('dp')
Inputs may be any that keep to these rules, and one draw needn't show every extreme that they name: `head_perm`: 0 pairs each half with itself, 1 pairs it with the other half. `block_mask`: entry a + b is the keep flag of block a of the queries with block b of the keys (b <= a).
All inputs are finite; a program needn't handle non-finite values.
Results may differ from a plain program's by a relative error of at most 0.015.
The roundings to bfloat16 on the way count: a program that leaves them out, or rounds other values in their place, can miss the bound.
Values may be sent and summed in bfloat16 or wider, within the bound.
No kernel may reach another device: no remote copies, remote signals or barrier semaphores. Data moves between devices by JAX's collectives and lax.ppermute only.
A program may use at most 256 MiB of HBM per device.

v0:
```python
import jax
import jax.numpy as jnp
from jax import lax
from jax.sharding import PartitionSpec as P

HD = 64


norm_eps = 1e-05
masked_fill = -1e30


def layer_norm(hidden, gain_vec, shift_vec):
    centered = hidden - jnp.mean(hidden, axis=-1, keepdims=True)
    variance = jnp.mean(centered * centered, axis=-1, keepdims=True)
    return centered * lax.rsqrt(variance + norm_eps) * gain_vec + shift_vec


def gelu_exact(values):
    return jax.nn.gelu(values, approximate=False)


def contract_rows(first_mat, second_mat):
    return lax.dot_general(
        first_mat, second_mat, (((0,), (0,)), ((), ())), preferred_element_type=jnp.float32
    )


def contract_cols(first_mat, second_mat):
    return lax.dot_general(
        first_mat, second_mat, (((1,), (1,)), ((), ())), preferred_element_type=jnp.float32
    )


def pair_pattern(mask_rows, half_len, block_len):
    blocks = jnp.arange(half_len) // block_len
    row_block = blocks[:, None]
    col_block = blocks[None, :]
    entry_index = row_block + col_block
    chosen = jnp.zeros((mask_rows.shape[0], half_len, half_len), dtype=jnp.bool_)
    for entry_id in range(3):
        chosen = (
            chosen | (mask_rows[:, entry_id, None, None] == 1) & (entry_index == entry_id)[None]
        )
    allowed = chosen & (col_block <= row_block)[None]
    allowed_f = allowed.astype(jnp.float32)
    dead_f = 1.0 - jnp.max(allowed_f, axis=-1)
    return (allowed, allowed_f, dead_f)


def pair_keys(values, swapped):
    return jnp.where(swapped[None, :, None], jnp.roll(values, values.shape[0] // 2, axis=0), values)


def split_pairs(proj_low, perm_seq, head_count):
    seq_len = proj_low.shape[0]
    half_len = seq_len // 2
    split_heads = proj_low.reshape(seq_len, 3, head_count, HD)
    swapped = perm_seq == 1
    query_pair = split_heads[:, 0].reshape(2, half_len, head_count, HD)
    key_pair = pair_keys(split_heads[:, 1], swapped).reshape(2, half_len, head_count, HD)
    value_pair = pair_keys(split_heads[:, 2], swapped).reshape(2, half_len, head_count, HD)
    return (query_pair, key_pair, value_pair, swapped)


def masked_scores(query_pair, key_pair, allowed):
    raw_scores = jnp.einsum(
        "iqhd,ikhd->ihqk", query_pair, key_pair, preferred_element_type=jnp.float32
    ) * HD ** (-0.5)
    return jnp.where(allowed[None], raw_scores, masked_fill)


def forward_pass(tokens_seq, perm_seq, mask_seq, weights):
    (
        w_qkv,
        b_qv,
        w_out,
        b_out,
        gain_one,
        shift_one,
        w_up,
        b_up,
        w_down,
        b_down,
        gain_two,
        shift_two,
    ) = weights
    seq_len = tokens_seq.shape[0]
    half_len = seq_len // 2
    local_width = w_qkv.shape[2]
    head_count = local_width // HD
    projected = jnp.einsum("td,dcf->tcf", tokens_seq, w_qkv, preferred_element_type=jnp.float32)
    bias_rows = jnp.stack([b_qv[0], jnp.zeros_like(b_qv[0]), b_qv[1]]).astype(jnp.float32)
    proj_low = (projected + bias_rows[None]).astype(jnp.bfloat16)
    query_pair, key_pair, value_pair, swapped = split_pairs(proj_low, perm_seq, head_count)
    allowed, allowed_f, dead_f = pair_pattern(mask_seq, half_len, half_len // 2)
    masked = masked_scores(query_pair, key_pair, allowed)
    row_max = jnp.max(masked, axis=-1)
    row_total = jnp.sum(jnp.exp(masked - row_max[..., None]) * allowed_f[None], axis=-1)
    log_total = row_max + jnp.log(row_total + dead_f[None])
    attn_weights = (jnp.exp(masked - log_total[..., None]) * allowed_f[None]).astype(jnp.bfloat16)
    context = jnp.einsum(
        "ihqk,ikhd->iqhd", attn_weights, value_pair, preferred_element_type=jnp.float32
    )
    context_low = context.reshape(seq_len, local_width).astype(jnp.bfloat16)
    attn_part = jnp.dot(context_low, w_out, preferred_element_type=jnp.float32)
    attn_out = lax.psum(attn_part, "mp")
    resid_one = tokens_seq.astype(jnp.float32) + attn_out + b_out.astype(jnp.float32)
    normed_one = layer_norm(resid_one, gain_one.astype(jnp.float32), shift_one.astype(jnp.float32))
    normed_share = normed_one.astype(jnp.bfloat16)
    pre_act = jnp.dot(normed_share, w_up, preferred_element_type=jnp.float32) + b_up.astype(
        jnp.float32
    )
    hidden_low = gelu_exact(pre_act).astype(jnp.bfloat16)
    ffn_part = jnp.dot(hidden_low, w_down, preferred_element_type=jnp.float32)
    ffn_out = lax.psum(ffn_part, "mp")
    resid_two = normed_one + ffn_out + b_down.astype(jnp.float32)
    out_rows = layer_norm(
        resid_two, gain_two.astype(jnp.float32), shift_two.astype(jnp.float32)
    ).astype(jnp.bfloat16)
    saved_state = (
        proj_low,
        log_total,
        context_low,
        resid_one,
        normed_share,
        pre_act,
        hidden_low,
        resid_two,
    )
    return (out_rows, saved_state)


def backward_pass(tokens_seq, cot_seq, perm_seq, mask_seq, saved_state, weights):
    w_qkv, w_out, gain_one, w_up, w_down, gain_two = weights
    proj_low, log_total, context_low, resid_one, normed_low, pre_act, hidden_low, resid_two = (
        saved_state
    )
    seq_len = tokens_seq.shape[0]
    half_len = seq_len // 2
    local_width = w_qkv.shape[2]
    head_count = local_width // HD
    gain_two_f = gain_two.astype(jnp.float32)
    _, norm_two_back = jax.vjp(layer_norm, resid_two, gain_two_f, jnp.zeros_like(gain_two_f))
    d_resid_two, g_gain_two, g_shift_two = norm_two_back(cot_seq.astype(jnp.float32))
    d_two_share = d_resid_two.astype(jnp.bfloat16)
    g_b_down = jnp.sum(d_resid_two, axis=0)
    g_w_down = contract_rows(hidden_low, d_two_share)
    d_hidden = contract_cols(d_two_share, w_down)
    _, gelu_back = jax.vjp(gelu_exact, pre_act)
    d_pre = gelu_back(d_hidden)[0].astype(jnp.bfloat16)
    g_b_up = jnp.sum(d_pre, axis=0, dtype=jnp.float32)
    g_w_up = contract_rows(normed_low, d_pre)
    d_normed_part = contract_cols(d_pre, w_up)
    d_normed_one = lax.psum(d_normed_part, "mp") + d_resid_two
    gain_one_f = gain_one.astype(jnp.float32)
    _, norm_one_back = jax.vjp(layer_norm, resid_one, gain_one_f, jnp.zeros_like(gain_one_f))
    d_resid_one, g_gain_one, g_shift_one = norm_one_back(d_normed_one)
    d_one_share = d_resid_one.astype(jnp.bfloat16)
    g_b_out = jnp.sum(d_resid_one, axis=0)
    g_w_out = contract_rows(context_low, d_one_share)
    d_context = contract_cols(d_one_share, w_out).astype(jnp.bfloat16)
    query_pair, key_pair, value_pair, swapped = split_pairs(proj_low, perm_seq, head_count)
    allowed, allowed_f, dead_f = pair_pattern(mask_seq, half_len, half_len // 2)
    masked = masked_scores(query_pair, key_pair, allowed)
    attn_prob = jnp.exp(masked - log_total[..., None]) * allowed_f[None]
    d_context_pair = d_context.reshape(2, half_len, head_count, HD)
    d_weights = jnp.einsum(
        "iqhd,ikhd->ihqk", d_context_pair, value_pair, preferred_element_type=jnp.float32
    )
    row_dot = jnp.sum(attn_prob * d_weights, axis=-1, keepdims=True)
    d_scores = (attn_prob * (d_weights - row_dot)).astype(jnp.bfloat16)
    score_scale = HD ** (-0.5)
    d_query = (
        jnp.einsum("ihqk,ikhd->iqhd", d_scores, key_pair, preferred_element_type=jnp.float32)
        * score_scale
    )
    d_key_pair = (
        jnp.einsum("ihqk,iqhd->ikhd", d_scores, query_pair, preferred_element_type=jnp.float32)
        * score_scale
    )
    d_value_pair = jnp.einsum(
        "ihqk,iqhd->ikhd",
        attn_prob.astype(jnp.bfloat16),
        d_context_pair,
        preferred_element_type=jnp.float32,
    )
    d_key = pair_keys(d_key_pair.reshape(seq_len, head_count, HD), swapped)
    d_value = pair_keys(d_value_pair.reshape(seq_len, head_count, HD), swapped)
    d_projected = jnp.stack(
        [
            d_query.reshape(seq_len, local_width),
            d_key.reshape(seq_len, local_width),
            d_value.reshape(seq_len, local_width),
        ],
        axis=1,
    ).astype(jnp.bfloat16)
    g_b_qv = jnp.stack(
        [
            jnp.sum(d_projected[:, 0], axis=0, dtype=jnp.float32),
            jnp.sum(d_projected[:, 2], axis=0, dtype=jnp.float32),
        ]
    )
    g_w_qkv = jnp.einsum("td,tcf->dcf", tokens_seq, d_projected, preferred_element_type=jnp.float32)
    d_input_part = jnp.einsum("tcf,dcf->td", d_projected, w_qkv, preferred_element_type=jnp.float32)
    input_seq = lax.psum(d_input_part.astype(jnp.bfloat16), "mp").astype(jnp.float32) + d_resid_one
    gradients = (
        g_w_qkv,
        g_b_qv,
        g_w_out,
        g_b_out,
        g_gain_one,
        g_shift_one,
        g_w_up,
        g_b_up,
        g_w_down,
        g_b_down,
        g_gain_two,
        g_shift_two,
    )
    return (input_seq, gradients)


def body(
    tokens,
    grad_out,
    head_perm,
    block_mask,
    w_qkv,
    b_qv,
    w_out,
    b_out,
    gain_one,
    shift_one,
    w_up,
    b_up,
    w_down,
    b_down,
    gain_two,
    shift_two,
):
    batch_count = head_perm.shape[0]
    seq_len = tokens.shape[0] // batch_count
    totals = None
    out_parts = []
    input_parts = []
    for batch_index in range(batch_count):
        row_start = batch_index * seq_len
        tokens_seq = tokens[row_start : row_start + seq_len]
        cot_seq = grad_out[row_start : row_start + seq_len]
        perm_seq = head_perm[batch_index]
        mask_seq = block_mask[batch_index]
        forward_weights = (
            lax.all_gather(w_qkv, "dp", axis=0, tiled=True),
            lax.all_gather(b_qv, "dp", axis=1, tiled=True),
            lax.all_gather(w_out, "dp", axis=1, tiled=True),
            lax.all_gather(b_out, "dp", axis=0, tiled=True),
            lax.all_gather(gain_one, "dp", axis=0, tiled=True),
            lax.all_gather(shift_one, "dp", axis=0, tiled=True),
            lax.all_gather(w_up, "dp", axis=0, tiled=True),
            lax.all_gather(b_up, "dp", axis=0, tiled=True),
            lax.all_gather(w_down, "dp", axis=1, tiled=True),
            lax.all_gather(b_down, "dp", axis=0, tiled=True),
            lax.all_gather(gain_two, "dp", axis=0, tiled=True),
            lax.all_gather(shift_two, "dp", axis=0, tiled=True),
        )
        out_seq, saved_state = forward_pass(tokens_seq, perm_seq, mask_seq, forward_weights)
        backward_weights = (
            lax.all_gather(w_qkv, "dp", axis=0, tiled=True),
            lax.all_gather(w_out, "dp", axis=1, tiled=True),
            lax.all_gather(gain_one, "dp", axis=0, tiled=True),
            lax.all_gather(w_up, "dp", axis=0, tiled=True),
            lax.all_gather(w_down, "dp", axis=1, tiled=True),
            lax.all_gather(gain_two, "dp", axis=0, tiled=True),
        )
        input_seq, gradients = backward_pass(
            tokens_seq, cot_seq, perm_seq, mask_seq, saved_state, backward_weights
        )
        if totals is None:
            totals = gradients
        else:
            totals = tuple((summed + latest for summed, latest in zip(totals, gradients)))
        out_parts.append(out_seq)
        input_parts.append(input_seq)
    (
        t_w_qkv,
        t_b_qv,
        t_w_out,
        t_b_out,
        t_gain_one,
        t_shift_one,
        t_w_up,
        t_b_up,
        t_w_down,
        t_b_down,
        t_gain_two,
        t_shift_two,
    ) = totals
    shards = (
        lax.psum_scatter(t_w_qkv, "dp", scatter_dimension=0, tiled=True),
        lax.psum_scatter(t_b_qv, "dp", scatter_dimension=1, tiled=True),
        lax.psum_scatter(t_w_out, "dp", scatter_dimension=1, tiled=True),
        lax.psum_scatter(t_b_out, "dp", scatter_dimension=0, tiled=True),
        lax.psum_scatter(t_gain_one, "dp", scatter_dimension=0, tiled=True),
        lax.psum_scatter(t_shift_one, "dp", scatter_dimension=0, tiled=True),
        lax.psum_scatter(t_w_up, "dp", scatter_dimension=0, tiled=True),
        lax.psum_scatter(t_b_up, "dp", scatter_dimension=0, tiled=True),
        lax.psum_scatter(t_w_down, "dp", scatter_dimension=1, tiled=True),
        lax.psum_scatter(t_b_down, "dp", scatter_dimension=0, tiled=True),
        lax.psum_scatter(t_gain_two, "dp", scatter_dimension=0, tiled=True),
        lax.psum_scatter(t_shift_two, "dp", scatter_dimension=0, tiled=True),
    )
    output = jnp.concatenate(out_parts, axis=0)
    input_grad = jnp.concatenate(input_parts, axis=0)
    return (
        output,
        input_grad,
        shards[0],
        shards[1],
        shards[2],
        shards[3],
        shards[4],
        shards[5],
        shards[6],
        shards[7],
        shards[8],
        shards[9],
        shards[10],
        shards[11],
    )


def solution(mesh):
    placed = (
        P("dp", None),
        P("dp", None),
        P("dp", "mp"),
        P("dp", "mp", None),
        P("dp", None, "mp"),
        P(None, ("mp", "dp")),
        P("mp", "dp"),
        P("dp"),
        P("dp"),
        P("dp"),
        P("dp", "mp"),
        P(("mp", "dp")),
        P("mp", "dp"),
        P("dp"),
        P("dp"),
        P("dp"),
    )
    return jax.shard_map(
        body,
        mesh=mesh,
        in_specs=placed,
        out_specs=(
            P("dp", None),
            P("dp", None),
            P("dp", None, "mp"),
            P(None, ("mp", "dp")),
            P("mp", "dp"),
            P("dp"),
            P("dp"),
            P("dp"),
            P("dp", "mp"),
            P(("mp", "dp")),
            P("mp", "dp"),
            P("dp"),
            P("dp"),
            P("dp"),
        ),
        check_vma=False,
    )
```

profile of v0, /device:TPU:0, one launch (start us, length us, event | category | flops | bytes accessed | tf_op | source)
XLA Modules:
  0.0 1341.1 jit_solution(12367896143275283011)
XLA Ops:
  8.7 23.3 %all-gather = bf16[16,24,2]{1,2,0:T(2,128)(2,1)S(1)} all-gather(bf16[1,24,2]{1,2,0:T(2,128)(2,1)} %bitcast.207), channel_id=1, replica_groups=mesh['dp'=16,'mp'=2] {'dp'}, dimensions={0}, use_global_device_ids=true | all-gather | bytes 1632 | tf_op jit(solution)/shard_map/all_gather | solution.py:255
  45.8 20.8 %all_gather.26 = bf16[384,768]{0,1:T(8,128)(2,1)} all-gather(bf16[384,48]{0,1:T(8,128)(2,1)S(1)} %copy-done.88), channel_id=1, replica_groups=mesh['dp'=16,'mp'=2] {'dp'}, dimensions={1}, use_global_device_ids=true | all-gather | bytes 626688 | tf_op jit(solution)/shard_map/all_gather | solution.py:256
  130.1 6.4 fusion.56
  165.4 59.2 %all-reduce.20 = (bf16[768]{0:T(1024)(128)(2,1)S(1)}, bf16[768]{0:T(1024)(128)(2,1)S(1)}, bf16[768]{0:T(1024)(128)(2,1)S(1)}, bf16[1536]{0:T(1024)(128)(2,1)S(1)...) all-reduce(bf16[768]{0:T(1024)(128)(2,1)S(1)} %dynamic-update-slice, ...), channel_id=1, replica_groups=mesh['dp'=16,'mp'=2] {'dp'}, use_global_device_ids=true, to_apply=%add | all-reduce | flops 6144 | bytes 24576
  224.6 87.3 %all-reduce.34.cloned.1.call-done = (f32[1024,768]{1,0:T(8,128)}, f32[1024,768]{1,0:T(8,128)}) async-done(((f32[1024,768]{1,0:T(8,128)}, f32[1024,768]{1,0:T(8,128)}), (f32[1024,768]{1,0:T(8,128)}, f32[1024,768]{1,0:T(8,128)})) %all-reduce.34.cloned.1.call-update) | async-done | bytes 6291472 | tf_op jit(solution)/shard_map/psum | solution.py:107
  318.7 37.9 %all-gather.7.cloned.1.call-done = bf16[768,1536]{1,0:T(8,128)(2,1)} async-done(((bf16[48,1536]{1,0:T(8,128)(2,1)}), bf16[768,1536]{1,0:T(8,128)(2,1)}) %all-gather.7.cloned.1.call-update) | async-done | bytes 2359312 | tf_op jit(solution)/shard_map/all_gather | solution.py:260
  364.8 31.7 %multiply_convert_fusion.3 = (bf16[1024,1536]{1,0:T(8,128)(2,1)}, f32[1024,1536]{1,0:T(8,128)}, bf16[1024,1536]{1,0:T(8,128)(2,1)}, f32[1024,1536]{1,0:T(8,128)}, f32[1024,1536]{1,0:T(8,128)}) fusion(f32[1536]{0:T(1024)S(1)} %convert_element_type.196, f32[1024,1536]{1,0:T(8,128)S(1)} %fusion.101, bf16[768,1536]{1,0:T(8,128)(2,1)S(1)} %copy-done.121, ...), kind=kOutput, calls=%fused_computation.34 | convolution fusion | flops 2627469312 | bytes 36982784 | tf_op jit(solution)/shard_map/dot_general | solution.py:111
  399.7 7.1 fusion.129
  411.3 152.0 %all-reduce.32.cloned.1.call-done = (f32[1024,768]{1,0:T(8,128)}, f32[1024,768]{1,0:T(8,128)}) async-done(((f32[1024,768]{1,0:T(8,128)}, f32[1024,768]{1,0:T(8,128)}), (f32[1024,768]{1,0:T(8,128)}, f32[1024,768]{1,0:T(8,128)})) %all-reduce.32.cloned.1.call-update) | async-done | bytes 6291472 | tf_op jit(solution)/shard_map/psum | solution.py:116
  578.0 10.6 convert_reduce_fusion.1
  593.0 7.3 convert_reduce_fusion
  608.3 151.4 %all-reduce.30.cloned.1.call-done = (f32[1024,768]{1,0:T(8,128)}, f32[1024,768]{1,0:T(8,128)}) async-done(((f32[1024,768]{1,0:T(8,128)}, f32[1024,768]{1,0:T(8,128)}), (f32[1024,768]{1,0:T(8,128)}, f32[1024,768]{1,0:T(8,128)})) %all-reduce.30.cloned.1.call-update) | async-done | bytes 6291472 | tf_op jit(solution)/shard_map/psum | solution.py:155
  759.8 5.6 multiply_reduce_fusion.4
  777.1 8.8 fusion.44
  797.3 9.8 fusion.41
  809.8 10.2 multiply_reduce_fusion
  820.0 10.3 multiply_convert_fusion
  836.3 10.1 multiply_reduce_fusion.1
  846.4 10.5 multiply_convert_fusion.1
  954.4 70.6 %all-reduce.28.cloned.1.call-done = f32[768,3,384]{2,1,0:T(4,128)} async-done(((f32[768,3,384]{2,1,0:T(4,128)}), f32[768,3,384]{2,1,0:T(4,128)}) %all-reduce.28.cloned.1.call-update) | async-done | bytes 3538960
  1026.8 86.3 %all-reduce.36.cloned.1.call-done = (bf16[1024,768]{1,0:T(8,128)(2,1)}, bf16[1024,768]{1,0:T(8,128)(2,1)}) async-done(((bf16[1024,768]{1,0:T(8,128)(2,1)}, bf16[1024,768]{1,0:T(8,128)(2,1)}), (bf16[1024,768]{1,0:T(8,128)(2,1)}, bf16[1024,768]{1,0:T(8,128)(2,1)})) %all-reduce.36.cloned.1.call-update) | async-done | bytes 3145744 | tf_op jit(solution)/shard_map/psum | solution.py:206
  1118.9 62.2 %all-reduce.16 = (f32[2,384]{1,0:T(2,128)S(1)}, f32[768]{0:T(1024)S(1)}, f32[768]{0:T(1024)S(1)}, f32[768]{0:T(1024)S(1)}, f32[1536]{0:T(1024)S(1)}, /*index=5*/...) all-reduce(f32[2,384]{1,0:T(2,128)S(1)} %maximum_add_fusion, ...), channel_id=3, replica_groups=mesh['dp'=16,'mp'=2] {'dp'}, use_global_device_ids=true, to_apply=%region_37.38.clone | all-reduce | flops 6912 | bytes 55296
  1193.5 79.0 %reduce-scatter.7.cloned.1.call-done = f32[48,1536]{1,0:T(8,128)} async-done(((f32[768,1536]{1,0:T(8,128)}), f32[48,1536]{1,0:T(8,128)}) %reduce-scatter.7.cloned.1.call-update) | async-done | bytes 294928 | tf_op jit(solution)/shard_map/reduce_scatter | solution.py:306
  1272.5 61.6 %reduce-scatter.5.cloned.1.call-done = f32[384,48]{0,1:T(8,128)} async-done(((f32[384,768]{0,1:T(8,128)}), f32[384,48]{0,1:T(8,128)}) %reduce-scatter.5.cloned.1.call-update) | async-done | bytes 73744 | tf_op jit(solution)/shard_map/reduce_scatter | solution.py:302
  (519 shorter events, 301.5 us)
Async XLA Ops:
  7.2 59.4 %all-gather.5.cloned.1.call-start = ((), (), s32[]{:S(2)}) async-start(), calls=%async_computation.3 | async-start | bytes 1880064 | tf_op jit(solution)/shard_map/all_gather | solution.py:254
  7.9 304.0 %all-reduce.34.cloned.1.call-start = ((), (), s32[]{:S(2)}) async-start(), calls=%async_computation.12 | async-start | bytes 12582912 | tf_op jit(solution)/shard_map/psum | solution.py:107
  37.3 91.7 %copy-start.2 = (pred[6,512,512]{1,2,0:T(8,128)(4,1)}, pred[6,512,512]{1,2,0:T(8,128)(4,1)S(1)}, u32[]{:S(2)}) copy-start(pred[6,512,512]{1,2,0:T(8,128)(4,1)S(1)} %get-tuple-element.124) | copy-start | bytes 4718596
  37.3 111.0 %copy-start.4 = (pred[6,512,512]{1,2,0:T(8,128)(4,1)}, pred[6,512,512]{1,2,0:T(8,128)(4,1)S(1)}, u32[]{:S(2)}) copy-start(pred[6,512,512]{1,2,0:T(8,128)(4,1)S(1)} %get-tuple-element.155) | copy-start | bytes 4718596
  160.4 196.1 %all-gather.7.cloned.1.call-start = ((), (), s32[]{:S(2)}) async-start(), calls=%async_computation.4 | async-start | bytes 2506752 | tf_op jit(solution)/shard_map/all_gather | solution.py:260
  161.2 238.6 %all-gather.9.cloned.1.call-start = ((), (), s32[]{:S(2)}) async-start(), calls=%async_computation.5 | async-start | bytes 2506752 | tf_op jit(solution)/shard_map/all_gather | solution.py:262
  161.8 401.5 %all-reduce.32.cloned.1.call-start = ((), (), s32[]{:S(2)}) async-start(), calls=%async_computation.11 | async-start | bytes 12582912 | tf_op jit(solution)/shard_map/psum | solution.py:116
  224.6 338.7 %copy-start.108 = (f32[768]{0:T(1024)}, f32[768]{0:T(1024)S(1)}, u32[]{:S(2)}) copy-start(f32[768]{0:T(1024)S(1)} %convert_element_type.194) | copy-start | bytes 9220
  316.6 448.8 %copy-start.7 = (f32[1024,768]{1,0:T(8,128)}, f32[1024,768]{1,0:T(8,128)S(1)}, u32[]{:S(2)}) copy-start(f32[1024,768]{1,0:T(8,128)S(1)} %get-tuple-element.118) | copy-start | bytes 9437188
  318.6 43.5 %copy-start.84 = (f32[1024]{0:T(1024)}, f32[1024]{0:T(1024)S(1)}, u32[]{:S(2)}) copy-start(f32[1024]{0:T(1024)S(1)} %multiply_reduce_fusion.11) | copy-start | bytes 12292
  318.7 446.7 %copy-start.81 = (f32[1024]{0:T(1024)}, f32[1024]{0:T(1024)S(1)}, u32[]{:S(2)}) copy-start(f32[1024]{0:T(1024)S(1)} %fusion.85) | copy-start | bytes 12292
  411.2 348.6 %all-reduce.30.cloned.1.call-start = ((), (), s32[]{:S(2)}) async-start(), calls=%async_computation.10 | async-start | bytes 12582912 | tf_op jit(solution)/shard_map/psum | solution.py:155
  573.7 19.2 %slice-start.8 = ((s8[6291456]{0:T(1024)(128)(4,1)}), s8[4194304]{0:T(1024)(128)(4,1)S(1)}, s32[]{:S(2)}) async-start(s8[6291456]{0:T(1024)(128)(4,1)} %bitcast.208), calls=%async_computation.22 | async-start | bytes 8388608
  578.0 15.0 %copy-start.24 = (f32[1024,768]{1,0:T(8,128)}, f32[1024,768]{1,0:T(8,128)S(1)}, u32[]{:S(2)}) copy-start(f32[1024,768]{1,0:T(8,128)S(1)} %get-tuple-element.110) | copy-start | bytes 9437188
  578.0 181.8 %copy-start.104 = (f32[1024]{0:T(1024)}, f32[1024]{0:T(1024)S(1)}, u32[]{:S(2)}) copy-start(f32[1024]{0:T(1024)S(1)} %negate_multiply_fusion.3) | copy-start | bytes 12292
  578.0 187.4 %copy-start.106 = (f32[1024]{0:T(1024)}, f32[1024]{0:T(1024)S(1)}, u32[]{:S(2)}) copy-start(f32[1024]{0:T(1024)S(1)} %negate_multiply_fusion.5) | copy-start | bytes 12292
  578.0 14.9 %slice-start.9 = ((s8[6291456]{0:T(1024)(128)(4,1)}), s8[2097152]{0:T(1024)(128)(4,1)S(1)}, s32[]{:S(2)}) async-start(s8[6291456]{0:T(1024)(128)(4,1)} %bitcast.208), calls=%async_computation.23 | async-start | bytes 4194304
  606.3 418.8 %all-reduce.28.cloned.1.call-start = ((), (), s32[]{:S(2)}) async-start(), calls=%async_computation.9 | async-start | bytes 9437184
  793.9 15.9 %slice-start.6 = ((s8[6291456]{0:T(1024)(128)(4,1)}), s8[2097152]{0:T(1024)(128)(4,1)S(1)}, s32[]{:S(2)}) async-start(s8[6291456]{0:T(1024)(128)(4,1)} %bitcast.186), calls=%async_computation.20 | async-start | bytes 4194304
  908.1 205.0 %all-reduce.36.cloned.1.call-start = ((), (), s32[]{:S(2)}) async-start(), calls=%async_computation.13 | async-start | bytes 6291456 | tf_op jit(solution)/shard_map/psum | solution.py:206
  918.1 275.4 %reduce-scatter.9.cloned.1.call-start = ((), (), s32[]{:S(2)}) async-start(), calls=%async_computation.8 | async-start | bytes 5013504 | tf_op jit(solution)/shard_map/reduce_scatter | solution.py:308
  929.8 342.7 %reduce-scatter.7.cloned.1.call-start = ((), (), s32[]{:S(2)}) async-start(), calls=%async_computation.7 | async-start | bytes 5013504 | tf_op jit(solution)/shard_map/reduce_scatter | solution.py:306
  941.6 392.5 %reduce-scatter.5.cloned.1.call-start = ((), (), s32[]{:S(2)}) async-start(), calls=%async_computation.6 | async-start | bytes 1253376 | tf_op jit(solution)/shard_map/reduce_scatter | solution.py:302
  1116.8 69.0 %copy-start.19 = (f32[1024,768]{1,0:T(8,128)S(1)}, f32[1024,768]{1,0:T(8,128)}, u32[]{:S(2)}) copy-start(f32[1024,768]{1,0:T(8,128)} %get-tuple-element.135) | copy-start | bytes 9437188
  (137 other events, 576.9 us)
Sparse Core Ops, SparseCore 0:
  10.3 43.1 all-gather.4
  160.6 151.2 all-reduce.33
  314.2 42.3 all-gather.6
  358.7 41.0 all-gather.8
  411.3 151.9 all-reduce.31
  606.5 153.2 all-reduce.29
  908.2 116.8 all-reduce.27
  1027.4 85.5 all-reduce.35
  1117.5 75.9 reduce-scatter.8
  1197.8 74.6 reduce-scatter.6
  1276.7 57.3 reduce-scatter.4
where the time goes:
time: 1350 us; the launch traced here: 1340 us
  waiting for transfers between devices  734 us (54%)
  matrix products  189 us (14%)
  blocking collectives  165 us (12%)
  local copies, waits for them, and re-layouts  128 us (9%)
  other arithmetic  104 us (8%)
  between operations  19.7 us (1%)
    psum x1, waiting for transfers between devices, forward_pass(): ffn_out = lax.psum(ffn_part, 'mp')  152 us
    psum x1, waiting for transfers between devices, backward_pass(): d_normed_one = lax.psum(d_normed_part, 'mp') + d_resid_two  151 us
    unnamed x2, blocking collectives  121 us
    psum x1, waiting for transfers between devices, forward_pass(): attn_out = lax.psum(attn_part, 'mp')  87.3 us
    psum x1, waiting for transfers between devices, backward_pass(): lax.psum(d_input_part.astype(jnp.bfloat16), 'mp').astype(jnp.float32)  86.3 us
    reduce_scatter x1, waiting for transfers between devices, body(): lax.psum_scatter(t_w_up, 'dp', scatter_dimension=0, tiled=True)  79 us
    unnamed x12, waiting for transfers between devices  72.7 us
    reduce_scatter x1, waiting for transfers between devices, body(): lax.psum_scatter(t_w_out, 'dp', scatter_dimension=1, tiled=True)  61.6 us
  transfers between devices with their start and end apart: 11, of which 10 were waited for; matrix products, arithmetic and copies ran while one was open for 9% of the time, Pallas kernels for 0%

commit v1 on v0

v1 whole, which is shorter than its diff:
```python
import functools

import jax
import jax.numpy as jnp
from jax import lax
from jax.experimental import pallas as pl
from jax.experimental.pallas import tpu as pltpu
from jax.sharding import PartitionSpec as P

HD = 64
PAIR = 2 * HD
BLOCK = 256
HALF = 2 * BLOCK
NORM_EPS = 1e-05
BF = jnp.bfloat16
F32 = jnp.float32
AXES = ("dp", "mp")
NN = (((1,), (0,)), ((), ()))
NT = (((1,), (1,)), ((), ()))
TN = (((0,), (0,)), ((), ()))
SMALL = 128


def mm(first, second, dims):
    return lax.dot_general(first, second, dims, preferred_element_type=F32)


def pairs_of(step):
    moves = []
    for d in range(16):
        for m in range(2):
            d2, m2 = step(d, m)
            moves.append((2 * d + m, 2 * d2 + m2))
    return moves


MOVE_X = pairs_of(lambda d, m: (d, 1 - m))
MOVE_Y = pairs_of(lambda d, m: (d ^ 2, m))
MOVE_CORE = pairs_of(lambda d, m: (d ^ 1, m))
MOVE_Z = [pairs_of(lambda d, m, k=k: ((d + 4 * k) % 16, m)) for k in (1, 2, 3)]
MOVE_FIRST = pairs_of(lambda d, m: (d ^ 2, m) if d & 1 else (d, 1 - m))
MOVE_SECOND = pairs_of(lambda d, m: (d, 1 - m) if d & 1 else (d ^ 2, m))


def move(values, moves):
    return lax.ppermute(values, AXES, moves)


def swap_mp(values):
    return lax.ppermute(values, "mp", [(0, 1), (1, 0)])


def assemble_kernel(where, *refs):
    pieces, (own_ref, other_ref), sem = refs[:8], refs[8:10], refs[10]
    rows = pieces[0].shape[1]
    z, y, core = where[0], where[1], where[2]
    z0, a0, b0, c0, z1, a1, b1, c1 = pieces
    first = core == 0

    def copies(ref, target, dy, dcore, slot):
        out = []
        for k in range(4):
            block = ((lax.rem(z + 4 - k, 4) * 2 + (y ^ dy)) * 2 + (core ^ dcore)) * rows
            out.append(
                pltpu.make_async_copy(
                    ref.at[k], target.at[pl.ds(pl.multiple_of(block, 16), rows), :], sem.at[slot, k]
                )
            )
        return out

    def both(cond, ref_if, ref_else, target, dy, dcore, slot):
        @pl.when(cond)
        def _():
            for copy in copies(ref_if, target, dy, dcore, slot):
                copy.start()

        @pl.when(jnp.logical_not(cond))
        def _():
            for copy in copies(ref_else, target, dy, dcore, slot):
                copy.start()

        return copies(ref_if, target, dy, dcore, slot)

    waits = []
    for slot, (ref, target, dy, dcore) in enumerate(
        ((z0, own_ref, 0, 0), (c0, other_ref, 1, 0), (z1, own_ref, 0, 1), (c1, other_ref, 1, 1))
    ):
        for copy in copies(ref, target, dy, dcore, slot):
            copy.start()
            waits.append(copy)
    waits += both(first, b0, a0, own_ref, 1, 0, 4)
    waits += both(first, a0, b0, other_ref, 0, 0, 5)
    waits += both(first, a1, b1, own_ref, 1, 1, 6)
    waits += both(first, b1, a1, other_ref, 0, 1, 7)
    for copy in waits:
        copy.wait()


def assemble(where, pieces):
    rows, cols = pieces[0].shape[1:]
    full = jax.ShapeDtypeStruct((16 * rows, cols), pieces[0].dtype)
    return pl.pallas_call(
        assemble_kernel,
        out_shape=(full, full),
        grid_spec=pltpu.PrefetchScalarGridSpec(
            num_scalar_prefetch=1,
            grid=(1,),
            in_specs=[pl.BlockSpec(memory_space=pl.ANY)] * 8,
            out_specs=[pl.BlockSpec((16 * rows, cols), lambda i, w: (0, 0))] * 2,
            scratch_shapes=[pltpu.SemaphoreType.DMA((8, 4))],
        ),
        cost_estimate=pl.CostEstimate(
            flops=0, transcendentals=0, bytes_accessed=64 * rows * cols * 2
        ),
        name="assemble",
    )(where, *pieces)


def gather(where, shard, dp_size):
    if dp_size != 16:
        full = lax.all_gather(shard, "dp", axis=0, tiled=True)
        return full, swap_mp(full)
    along_z = jnp.stack([shard] + [move(shard, moves) for moves in MOVE_Z])
    a = move(along_z, MOVE_FIRST)
    b = move(along_z, MOVE_SECOND)
    c = move(a, MOVE_SECOND)
    pieces = [along_z, a, b, c]
    pieces += [move(piece, MOVE_CORE) for piece in pieces]
    return assemble(where, pieces)


def split_kernel(where, own_ref, other_ref, keep_ref, send_ref, sem):
    rows = keep_ref.shape[3]
    z, y, core = where[0], where[1], where[2]
    copies = []
    for dcore, target in enumerate((keep_ref, send_ref)):
        for dy in range(2):
            for dm, source in enumerate((own_ref, other_ref)):
                for k in range(4):
                    block = ((lax.rem(z + k, 4) * 2 + (y ^ dy)) * 2 + (core ^ dcore)) * rows
                    copies.append(
                        pltpu.make_async_copy(
                            source.at[pl.ds(pl.multiple_of(block, 16), rows), :],
                            target.at[dy, dm, k],
                            sem.at[len(copies)],
                        )
                    )
    for copy in copies:
        copy.start()
    for copy in copies:
        copy.wait()


def split(where, own, other):
    rows, cols = own.shape[0] // 16, own.shape[1]
    part = jax.ShapeDtypeStruct((2, 2, 4, rows, cols), own.dtype)
    return pl.pallas_call(
        split_kernel,
        out_shape=(part, part),
        grid_spec=pltpu.PrefetchScalarGridSpec(
            num_scalar_prefetch=1,
            grid=(1,),
            in_specs=[pl.BlockSpec((16 * rows, cols), lambda i, w: (0, 0))] * 2,
            out_specs=[pl.BlockSpec(memory_space=pl.ANY)] * 2,
            scratch_shapes=[pltpu.SemaphoreType.DMA((32,))],
        ),
        cost_estimate=pl.CostEstimate(
            flops=0, transcendentals=0, bytes_accessed=64 * rows * cols * 2
        ),
        name="split",
    )(where, own, other)


def reduce_scatter(where, own, other, dp_size):
    if dp_size != 16:
        summed = own.astype(F32) + swap_mp(other).astype(F32)
        return lax.psum_scatter(summed, "dp", scatter_dimension=0, tiled=True)

    def add(first, second):
        return (first.astype(F32) + second.astype(F32)).astype(BF)

    keep, send = split(where, own, other)
    got = move(send, MOVE_CORE)
    send = add(keep[1], got[1])
    keep = add(keep[0], got[0])
    got = move(send, MOVE_Y)
    send = add(keep[1], got[1])
    keep = add(keep[0], got[0])
    got = move(send, MOVE_X)
    parts = [add(keep[k], got[k]) for k in range(1, 4)]
    total = keep[0].astype(F32) + got[0].astype(F32)
    for part, moves in zip(parts, MOVE_Z):
        total = total + move(part, moves).astype(F32)
    return total


def lane_mask(head, rows):
    lanes = lax.broadcasted_iota(jnp.int32, (rows, PAIR), 1)
    return (lanes < HD) if head == 0 else (lanes >= HD)


def attn_fwd_kernel(table, q_ref, k_ref, v_ref, ctx_ref, prob_ref):
    pair = pl.program_id(0)
    lanes = lax.broadcasted_iota(jnp.int32, (1, HALF), 1)
    for half in range(2):
        rows = pl.ds(half * HALF, HALF)
        query = q_ref[rows, :] * jnp.asarray(HD**-0.5, BF)
        parts = []
        for head in range(2):
            at = (pair * 2 + head) * 4
            start = (half ^ table[at]) * HALF
            flags = [table[at + 1 + n] == 1 for n in range(3)]
            key_lo = k_ref[pl.ds(pl.multiple_of(start, BLOCK), BLOCK), :]
            key_hi = k_ref[pl.ds(pl.multiple_of(start + BLOCK, BLOCK), BLOCK), :]
            masked = jnp.where(lane_mask(head, HALF), query, jnp.zeros_like(query))
            score_lo = mm(key_lo, masked, NT)
            score_hi = mm(key_hi, masked[BLOCK:], NT)
            no_lo = jnp.where(
                lanes < BLOCK,
                jnp.where(flags[0], 0.0, -1e30),
                jnp.where(flags[1], 0.0, -1e30),
            ).astype(F32)
            no_hi = jnp.where(flags[2], 0.0, -1e30).astype(F32)
            top_lo = jnp.max(score_lo, axis=0, keepdims=True) + no_lo
            top_hi = jnp.max(score_hi, axis=0, keepdims=True) + no_hi
            top = jnp.concatenate(
                [top_lo[:, :BLOCK], jnp.maximum(top_lo[:, BLOCK:], top_hi)], axis=1
            )
            ref_lo = jnp.where(no_lo < 0.0, 1e30, top)
            ref_hi = jnp.where(no_hi < 0.0, 1e30, top[:, BLOCK:])
            exp_lo = jnp.exp(score_lo - ref_lo)
            exp_hi = jnp.exp(score_hi - ref_hi)
            sum_lo = jnp.sum(exp_lo, axis=0, keepdims=True)
            sum_hi = jnp.sum(exp_hi, axis=0, keepdims=True)
            total = jnp.concatenate([sum_lo[:, :BLOCK], sum_lo[:, BLOCK:] + sum_hi], axis=1)
            scale = jnp.where(total > 0.0, 1.0 / jnp.where(total > 0.0, total, 1.0), 0.0)
            prob_lo = (exp_lo * scale).astype(BF)
            prob_hi = (exp_hi * scale[:, BLOCK:]).astype(BF)
            prob_ref[0, head, half, :, :HALF] = prob_lo
            prob_ref[0, head, half, :, HALF:] = prob_hi
            val_lo = v_ref[pl.ds(pl.multiple_of(start, BLOCK), BLOCK), :].T
            val_hi = v_ref[pl.ds(pl.multiple_of(start + BLOCK, BLOCK), BLOCK), :].T
            side = slice(head * HD, (head + 1) * HD)
            out_lo = mm(val_lo[side], prob_lo, NN)
            out_hi = mm(val_hi[side], prob_hi, NN)
            parts.append(
                jnp.concatenate([out_lo[:, :BLOCK], out_lo[:, BLOCK:] + out_hi], axis=1)
            )
        ctx_ref[rows, :] = jnp.concatenate(parts, axis=0).T.astype(BF)


def attn_fwd(table, proj):
    seq, width = proj.shape
    pairs = width // 3 // PAIR
    return pl.pallas_call(
        attn_fwd_kernel,
        out_shape=(
            jax.ShapeDtypeStruct((seq, width // 3), BF),
            jax.ShapeDtypeStruct((pairs, 2, 2, BLOCK, HALF + BLOCK), BF),
        ),
        grid_spec=pltpu.PrefetchScalarGridSpec(
            num_scalar_prefetch=1,
            grid=(pairs,),
            in_specs=[
                pl.BlockSpec((seq, PAIR), lambda p, t: (0, p)),
                pl.BlockSpec((seq, PAIR), lambda p, t: (0, p + pairs)),
                pl.BlockSpec((seq, PAIR), lambda p, t: (0, p + 2 * pairs)),
            ],
            out_specs=[
                pl.BlockSpec((seq, PAIR), lambda p, t: (0, p)),
                pl.BlockSpec((1, 2, 2, BLOCK, HALF + BLOCK), lambda p, t: (p, 0, 0, 0, 0)),
            ],
        ),
        cost_estimate=pl.CostEstimate(
            flops=pairs * 4 * 2 * 2 * 3 * BLOCK * BLOCK * PAIR,
            transcendentals=pairs * 4 * 3 * BLOCK * BLOCK,
            bytes_accessed=pairs * 4 * 3 * BLOCK * BLOCK * 2 + seq * width * 3,
        ),
        name="attn_fwd",
    )(table, proj, proj, proj)


def attn_bwd_kernel(table, q_ref, k_ref, v_ref, d_ref, prob_ref, dq_ref, dk_ref, dv_ref, k_acc, v_acc):
    pair = pl.program_id(0)
    for half in range(2):
        rows = pl.ds(half * HALF, HALF)
        query = q_ref[rows, :] * jnp.asarray(HD**-0.5, BF)
        d_ctx = d_ref[rows, :]
        parts = []
        for head in range(2):
            at = (pair * 2 + head) * 4
            start = (half ^ table[at]) * HALF
            at_lo = pl.ds(pl.multiple_of(start, BLOCK), BLOCK)
            at_hi = pl.ds(pl.multiple_of(start + BLOCK, BLOCK), BLOCK)
            keep = lane_mask(head, HALF)
            query_h = jnp.where(keep, query, jnp.zeros_like(query))
            d_ctx_h = jnp.where(keep, d_ctx, jnp.zeros_like(d_ctx))
            prob_lo = prob_ref[0, head, half, :, :HALF]
            prob_hi = prob_ref[0, head, half, :, HALF:]
            d_w_lo = mm(v_ref[at_lo, :], d_ctx_h, NT)
            d_w_hi = mm(v_ref[at_hi, :], d_ctx_h[BLOCK:], NT)
            wide_lo = prob_lo.astype(F32)
            wide_hi = prob_hi.astype(F32)
            dot_lo = jnp.sum(wide_lo * d_w_lo, axis=0, keepdims=True)
            dot_hi = jnp.sum(wide_hi * d_w_hi, axis=0, keepdims=True)
            dot = jnp.concatenate([dot_lo[:, :BLOCK], dot_lo[:, BLOCK:] + dot_hi], axis=1)
            d_s_lo = (wide_lo * (d_w_lo - dot)).astype(BF)
            d_s_hi = (wide_hi * (d_w_hi - dot[:, BLOCK:])).astype(BF)
            dk_lo = mm(d_s_lo, query_h, NN)
            dk_hi = mm(d_s_hi, query_h[BLOCK:], NN)
            dv_lo = mm(prob_lo, d_ctx_h, NN)
            dv_hi = mm(prob_hi, d_ctx_h[BLOCK:], NN)
            k_acc[head, at_lo, :] = dk_lo
            k_acc[head, at_hi, :] = dk_hi
            v_acc[head, at_lo, :] = dv_lo
            v_acc[head, at_hi, :] = dv_hi
            key_lo = k_ref[at_lo, :].T
            key_hi = k_ref[at_hi, :].T
            side = slice(head * HD, (head + 1) * HD)
            dq_lo = mm(key_lo[side], d_s_lo, NN)
            dq_hi = mm(key_hi[side], d_s_hi, NN)
            parts.append(jnp.concatenate([dq_lo[:, :BLOCK], dq_lo[:, BLOCK:] + dq_hi], axis=1))
        dq_ref[rows, :] = (jnp.concatenate(parts, axis=0).T * HD**-0.5).astype(BF)
    dk_ref[...] = (k_acc[0] + k_acc[1]).astype(BF)
    dv_ref[...] = (v_acc[0] + v_acc[1]).astype(BF)


def attn_bwd(table, proj, d_context, probs):
    seq, width = proj.shape
    pairs = width // 3 // PAIR
    part = jax.ShapeDtypeStruct((seq, width // 3), BF)
    column = pl.BlockSpec((seq, PAIR), lambda p, t: (0, p))
    return pl.pallas_call(
        attn_bwd_kernel,
        out_shape=(part, part, part),
        grid_spec=pltpu.PrefetchScalarGridSpec(
            num_scalar_prefetch=1,
            grid=(pairs,),
            in_specs=[
                column,
                pl.BlockSpec((seq, PAIR), lambda p, t: (0, p + pairs)),
                pl.BlockSpec((seq, PAIR), lambda p, t: (0, p + 2 * pairs)),
                column,
                pl.BlockSpec((1, 2, 2, BLOCK, HALF + BLOCK), lambda p, t: (p, 0, 0, 0, 0)),
            ],
            out_specs=[column] * 3,
            scratch_shapes=[pltpu.VMEM((2, seq, PAIR), F32)] * 2,
        ),
        cost_estimate=pl.CostEstimate(
            flops=pairs * 4 * 4 * 2 * 3 * BLOCK * BLOCK * PAIR,
            transcendentals=0,
            bytes_accessed=pairs * 4 * 3 * BLOCK * BLOCK * 2 + seq * width * 5,
        ),
        name="attn_bwd",
    )(table, proj, proj, proj, d_context, probs)


def norm_parts(values):
    centered = values - jnp.mean(values, axis=-1, keepdims=True)
    inverse = lax.rsqrt(jnp.mean(centered * centered, axis=-1, keepdims=True) + NORM_EPS)
    return centered * inverse, inverse


def norm_back(d_normed, z, inverse, gain):
    dz = d_normed * gain
    return (
        dz - jnp.mean(dz, axis=-1, keepdims=True) - z * jnp.mean(dz * z, axis=-1, keepdims=True)
    ) * inverse


def gelu_both(values):
    half = 0.5 * (1.0 + lax.erf(values * (0.5**0.5)))
    slope = half + values * jnp.exp(-0.5 * values * values) * 0.3989422804014327
    return values * half, slope


def body(
    dp_size,
    tokens,
    grad_out,
    head_perm,
    block_mask,
    w_qkv,
    b_qv,
    w_out,
    b_out,
    gain_one,
    shift_one,
    w_up,
    b_up,
    w_down,
    b_down,
    gain_two,
    shift_two,
):
    seq = tokens.shape[0] // head_perm.shape[0]
    rows = w_qkv.shape[0]
    width = w_qkv.shape[2]
    d_model = tokens.shape[1]
    dp_at = lax.axis_index("dp")
    mp_at = lax.axis_index("mp")
    where = jnp.stack([dp_at // 4, (dp_at // 2) % 2, dp_at % 2]).astype(jnp.int32)

    own_tokens = lax.dynamic_slice_in_dim(tokens, mp_at * seq, seq, 0)
    own_grad = lax.dynamic_slice_in_dim(grad_out, mp_at * seq, seq, 0)
    table = jnp.concatenate([head_perm[:, :, None], block_mask], axis=2).astype(jnp.int32)
    table = table.reshape(2, -1)
    table_own = lax.dynamic_index_in_dim(table, mp_at, 0, keepdims=False)
    table_other = swap_mp(lax.dynamic_index_in_dim(table, 1 - mp_at, 0, keepdims=False))

    small = jnp.stack(
        [
            b_out,
            gain_one,
            shift_one,
            b_down,
            gain_two,
            shift_two,
            b_up[:rows],
            b_up[rows:],
            b_qv.reshape(-1),
        ],
        axis=1,
    )
    small = jnp.pad(small, ((0, 0), (0, SMALL - small.shape[1])))
    shard_qkv = jnp.concatenate([w_qkv.reshape(rows, 3 * width), small], axis=1)
    qkv_own, qkv_other = gather(where, shard_qkv, dp_size)
    shard_up = jnp.concatenate([w_out.T, w_up], axis=1)
    up_own, up_other = gather(where, shard_up, dp_size)
    down_own, down_other = gather(where, w_down.T, dp_size)

    small_own = qkv_own[:, 3 * width :].astype(F32)
    small_other = qkv_other[:, 3 * width :].astype(F32)
    vectors = small_own.T
    b_out_f, gain_one_f, shift_one_f, b_down_f, gain_two_f, shift_two_f = (
        vectors[n][None] for n in range(6)
    )

    def up_bias(columns):
        return columns[:, 6:8].reshape(dp_size, rows, 2).transpose(0, 2, 1).reshape(1, -1)

    def qkv_bias(columns):
        parts = columns[:, 8].reshape(dp_size, 2, rows // 2).transpose(1, 0, 2).reshape(2, -1)
        return jnp.concatenate([parts[0], jnp.zeros_like(parts[0]), parts[1]])[None]

    wq = (qkv_own[:, : 3 * width], qkv_other[:, : 3 * width])
    wo = (up_own[:, :width], up_other[:, :width])
    wu = (up_own[:, width:], up_other[:, width:])
    wd = (down_own, down_other)

    proj = tuple(
        (mm(own_tokens, w, NN) + qkv_bias(s)).astype(BF)
        for w, s in zip(wq, (small_own, small_other))
    )
    tables = (table_own, table_other)
    ctx, probs = zip(*(attn_fwd(t, p) for t, p in zip(tables, proj)))
    attn_out = mm(ctx[0], wo[0], NT) + mm(ctx[1], wo[1], NT)
    resid_one = own_tokens.astype(F32) + attn_out + b_out_f
    z_one, inv_one = norm_parts(resid_one)
    normed_one = z_one * gain_one_f + shift_one_f
    normed_low = normed_one.astype(BF)
    hidden, slope = [], []
    for w, s in zip(wu, (small_own, small_other)):
        pre = mm(normed_low, w, NN) + up_bias(s)
        gelu, grad = gelu_both(pre)
        hidden.append(gelu.astype(BF))
        slope.append(grad.astype(BF))
    ffn_out = mm(hidden[0], wd[0], NT) + mm(hidden[1], wd[1], NT)
    resid_two = normed_one + ffn_out + b_down_f
    z_two, inv_two = norm_parts(resid_two)
    out_own = (z_two * gain_two_f + shift_two_f).astype(BF)
    out_other = swap_mp(out_own)

    cot = own_grad.astype(F32)
    g_gain_two = jnp.sum(cot * z_two, axis=0)
    g_shift_two = jnp.sum(cot, axis=0)
    d_two = norm_back(cot, z_two, inv_two, gain_two_f)
    d_two_low = d_two.astype(BF)
    g_b_down = jnp.sum(d_two, axis=0)
    g_down = [mm(d_two_low, h, TN).astype(BF) for h in hidden]
    s_down = reduce_scatter(where, *g_down, dp_size)
    d_pre = [(mm(d_two_low, w, NN) * s.astype(F32)).astype(BF) for w, s in zip(wd, slope)]
    g_b_up = [jnp.sum(d, axis=0, dtype=F32) for d in d_pre]
    g_up = [mm(normed_low, d, TN).astype(BF) for d in d_pre]
    d_normed = mm(d_pre[0], wu[0], NT) + mm(d_pre[1], wu[1], NT) + d_two
    g_gain_one = jnp.sum(d_normed * z_one, axis=0)
    g_shift_one = jnp.sum(d_normed, axis=0)
    d_one = norm_back(d_normed, z_one, inv_one, gain_one_f)
    d_one_low = d_one.astype(BF)
    g_b_out = jnp.sum(d_one, axis=0)
    g_out = [mm(d_one_low, c, TN).astype(BF) for c in ctx]
    s_up = reduce_scatter(
        where, *(jnp.concatenate([o, u], axis=1) for o, u in zip(g_out, g_up)), dp_size
    )
    d_ctx = [mm(d_one_low, w, NN).astype(BF) for w in wo]
    d_proj = [
        jnp.concatenate(attn_bwd(t, p, d, pr), axis=1)
        for t, p, d, pr in zip(tables, proj, d_ctx, probs)
    ]
    d_input = mm(d_proj[0], wq[0], NT) + mm(d_proj[1], wq[1], NT) + d_one
    in_other = swap_mp(d_input.astype(BF)).astype(F32)
    g_qkv = [mm(own_tokens, d, TN).astype(BF) for d in d_proj]

    shared = jnp.stack([g_b_out, g_gain_one, g_shift_one, g_b_down, g_gain_two, g_shift_two])

    def small_grads(g_up_bias, d):
        sums = jnp.sum(d, axis=0, dtype=F32)
        qv = jnp.stack([sums[:width], sums[2 * width :]]).reshape(2, dp_size, rows // 2)
        per_up = g_up_bias.reshape(dp_size, 2, rows).transpose(1, 0, 2).reshape(2, d_model)
        stacked = jnp.concatenate(
            [shared, per_up, qv.transpose(1, 0, 2).reshape(1, d_model)], axis=0
        )
        return jnp.pad(stacked, ((0, SMALL - stacked.shape[0]), (0, 0))).T.astype(BF)

    s_qkv = reduce_scatter(
        where,
        *(
            jnp.concatenate([g, small_grads(b, d)], axis=1)
            for g, b, d in zip(g_qkv, g_b_up, d_proj)
        ),
        dp_size,
    )

    def place(own, other):
        whole = jnp.zeros((2 * seq, d_model), own.dtype)
        whole = lax.dynamic_update_slice_in_dim(whole, own, mp_at * seq, 0)
        return lax.dynamic_update_slice_in_dim(whole, other, (1 - mp_at) * seq, 0)

    cols = s_qkv[:, 3 * width :].T
    return (
        place(out_own, out_other),
        place(d_input, in_other),
        s_qkv[:, : 3 * width].reshape(rows, 3, width),
        cols[8].reshape(2, rows // 2),
        s_up[:, :width].T,
        cols[0],
        cols[1],
        cols[2],
        s_up[:, width:],
        cols[6:8].reshape(-1),
        s_down.T,
        cols[3],
        cols[4],
        cols[5],
    )


def solution(mesh):
    placed = (
        P("dp", None),
        P("dp", None),
        P("dp", "mp"),
        P("dp", "mp", None),
        P("dp", None, "mp"),
        P(None, ("mp", "dp")),
        P("mp", "dp"),
        P("dp"),
        P("dp"),
        P("dp"),
        P("dp", "mp"),
        P(("mp", "dp")),
        P("mp", "dp"),
        P("dp"),
        P("dp"),
        P("dp"),
    )
    return jax.shard_map(
        functools.partial(body, mesh.shape["dp"]),
        mesh=mesh,
        in_specs=placed,
        out_specs=(
            P("dp", None),
            P("dp", None),
            P("dp", None, "mp"),
            P(None, ("mp", "dp")),
            P("mp", "dp"),
            P("dp"),
            P("dp"),
            P("dp"),
            P("dp", "mp"),
            P(("mp", "dp")),
            P("mp", "dp"),
            P("dp"),
            P("dp"),
            P("dp"),
        ),
        check_vma=False,
    )
```

time: 1350 us -> 486 us (0.36)
  waiting for transfers between devices: 734 us -> 145 us
  blocking collectives: 165 us -> 0 us
  matrix products: 189 us -> 97.1 us
  local copies, waits for them, and re-layouts: 128 us -> 51.5 us
  Pallas kernels: 0 us -> 73.6 us
  starting transfers between devices: 0.7 us -> 60 us
  other arithmetic: 104 us -> 48.4 us
  between operations: 19.7 us -> 2.17 us
    psum x4 -> x0, waiting for transfers between devices: 477 us -> none  [the longest x1 152 us: forward_pass(): ffn_out = lax.psum(ffn_part, 'mp')]
    ppermute x0 -> x51, waiting for transfers between devices: none -> 145 us  [the longest x48 93 us: move(): return lax.ppermute(values, AXES, moves)]
    reduce_scatter x3 -> x0, waiting for transfers between devices: 143 us -> none  [the longest x1 79 us: body(): lax.psum_scatter(t_w_up, 'dp', scatter_dimension=0, tiled=True)]
    unnamed x2 -> x0, blocking collectives: 121 us -> none
    dot_general x36 -> x24, matrix products: 189 us -> 97.1 us  [mm(): return lax.dot_general(first, second, dims, preferred_element_type=F32)]
    pallas_call x0 -> x10, Pallas kernels: none -> 73.6 us  [the longest x2 22 us: attn_bwd(): pl.pallas_call(attn_bwd_kernel, out_shape=(part, part, part), grid_spec=p...]
    unnamed x12 -> x0, waiting for transfers between devices: 72.7 us -> none
    ppermute x0 -> x51, starting transfers between devices: none -> 60 us  [the longest x48 56.7 us: move(): return lax.ppermute(values, AXES, moves)]
  transfers between devices with their start and end apart: 11 -> 51, of which waited for: 10 -> 15; matrix products, arithmetic and copies ran while one was open for 9% -> 18% of each run, Pallas kernels for 0% -> 8%
where the time goes in v1:
time: 486 us; the launch traced here: 478 us
  waiting for transfers between devices  145 us (30%)
  matrix products  97.1 us (20%)
  Pallas kernels  73.6 us (15%)
  starting transfers between devices  60 us (12%)
  local copies, waits for them, and re-layouts  51.5 us (11%)
  other arithmetic  48.4 us (10%)
    dot_general x24, matrix products, mm(): return lax.dot_general(first, second, dims, preferred_element_type=F32)  97.1 us
    ppermute x48, waiting for transfers between devices, move(): return lax.ppermute(values, AXES, moves)  93 us
    ppermute x48, starting transfers between devices, move(): return lax.ppermute(values, AXES, moves)  56.7 us
    ppermute x3, waiting for transfers between devices, swap_mp(): return lax.ppermute(values, 'mp', [(0, 1), (1, 0)])  52.3 us
    pallas_call x2, Pallas kernels, attn_bwd(): pl.pallas_call(attn_bwd_kernel, out_shape=(part, part, part), grid_spec=p...  22 us
    unnamed x81, local copies, waits for them, and re-layouts  21.1 us
    pallas_call x2, Pallas kernels, attn_fwd(): pl.pallas_call(attn_fwd_kernel, out_shape=(jax.ShapeDtypeStruct((seq, wid...  18.1 us
    pallas_call x3, Pallas kernels, assemble(): pl.pallas_call(assemble_kernel, out_shape=(full, full), grid_spec=pltpu.P...  16.9 us
  transfers between devices with their start and end apart: 51, of which 15 were waited for; matrix products, arithmetic and copies ran while one was open for 18% of the time, Pallas kernels for 8%

profile of v1, /device:TPU:0, one launch (start us, length us, event | category | flops | bytes accessed | tf_op | source)
XLA Modules:
  0.0 478.1 jit_solution(6272652026260020203)
XLA Ops:
  31.2 6.2 %collective-permute-start.10 = (bf16[48,1920]{1,0:T(8,128)(2,1)S(1)}, bf16[48,1920]{1,0:T(8,128)(2,1)}, u32[]{:S(2)}, u32[]{:S(2)}) collective-permute-start(bf16[48,1920]{1,0:T(8,128)(2,1)S(1)} %get-tuple-element.169), channel_id=1, source_target_pairs={{0,8},{1,9},{2,10},{3,11},{4,12},{5,13},{6,14},{7,15},{8,16},{9,17... | collective-permute-start | bytes 552968 | tf_op jit(solution)/shard_map/ppermute | solution.py:46
  62.0 5.0 %assemble.3 = (bf16[768,1280]{1,0:T(8,128)(2,1)}, bf16[768,1280]{1,0:T(8,128)(2,1)}) custom-call(s32[3]{0:T(128)} %pad_add_fusion.1.where, bf16[4,48,1280]{2,1,0:T(8,128)(2,1)} %pad_maximum_fusion.6.refs_0_, bf16[4,48,1280]{2,1,0:T(8,128)(2,1)} %collective-permute-done.3.refs_1_, bf16[4,48,1280]{2,1,0:T(8,128)(2,1)} %collective-permute-done.4.refs_2_, ...), custom_call_target="tpu_custom_call" | custom-call | bytes 7864320 | tf_op jit(solution)/shard_map/assemble/pallas_call | solution.py:102
  71.7 18.5 %collective-permute-done.13.refs_1_ = bf16[4,48,1920]{2,1,0:T(8,128)(2,1)} collective-permute-done((bf16[4,48,1920]{2,1,0:T(8,128)(2,1)}, bf16[4,48,1920]{2,1,0:T(8,128)(2,1)}, u32[]{:S(2)}, u32[]{:S(2)}) %collective-permute-start.13) | collective-permute-done | bytes 737312 | tf_op jit(solution)/shard_map/ppermute | solution.py:46
  92.9 5.7 %add_convert_fusion.1.q_ref.k_ref.v_ref = bf16[1024,1152]{1,0:T(8,128)(2,1)} fusion(bf16[1024,768]{1,0:T(8,128)(2,1)} %constant_dynamic-slice_fusion.3, f32[1152]{0:T(1024)S(1)} %get-tuple-element.176, bf16[768,1280]{1,0:T(8,128)(2,1)} %get-tuple-element.36), kind=kOutput, calls=%fused_computation.19 | convolution fusion | flops 1814298624 | bytes 5706240 | tf_op jit(solution)/shard_map/dot_general | solution.py:25
  98.5 9.2 %attn_fwd.2 = (bf16[1024,384]{1,0:T(8,128)(2,1)}, bf16[3,2,2,256,768]{4,3,2,1,0:T(8,128)(2,1)}) custom-call(s32[24]{0:T(128)} %get-tuple-element.178.table, bf16[1024,1152]{1,0:T(8,128)(2,1)} %add_convert_fusion.1.q_ref.k_ref.v_ref, bf16[1024,1152]{1,0:T(8,128)(2,1)} %add_convert_fusion.1.q_ref.k_ref.v_ref, ...), custom_call_target="tpu_custom_call" | custom-call | flops 1207959552 | bytes 8257536 | tf_op jit(solution)/shard_map/attn_fwd/pallas_call | solution.py:255
  109.4 5.5 %add_convert_fusion.q_ref.k_ref.v_ref = bf16[1024,1152]{1,0:T(8,128)(2,1)} fusion(bf16[1024,768]{1,0:T(8,128)(2,1)} %constant_dynamic-slice_fusion.3, f32[1152]{0:T(1024)S(1)} %get-tuple-element.177, bf16[768,1280]{1,0:T(8,128)(2,1)} %get-tuple-element.39), kind=kOutput, calls=%fused_computation.18 | convolution fusion | flops 1814298624 | bytes 5706240 | tf_op jit(solution)/shard_map/dot_general | solution.py:25
  114.9 8.9 %attn_fwd.3 = (bf16[1024,384]{1,0:T(8,128)(2,1)}, bf16[3,2,2,256,768]{4,3,2,1,0:T(8,128)(2,1)}) custom-call(s32[24]{0:T(128)} %copy-done.29, bf16[1024,1152]{1,0:T(8,128)(2,1)} %add_convert_fusion.q_ref.k_ref.v_ref, bf16[1024,1152]{1,0:T(8,128)(2,1)} %add_convert_fusion.q_ref.k_ref.v_ref, bf16[1024,1152]{1,0:T(8,128)(2,1)} %add_convert_fusion.q_ref.k_ref.v_ref), custom_call_target="tpu_custom_call" | custom-call | flops 1207959552 | bytes 8257536 | tf_op jit(solution)/shard_map/attn_fwd/pallas_call | solution.py:255
  125.1 5.6 %assemble.5 = (bf16[768,1536]{1,0:T(8,128)(2,1)}, bf16[768,1536]{1,0:T(8,128)(2,1)}) custom-call(s32[3]{0:T(128)} %pad_add_fusion.1.where, bf16[4,48,1536]{2,1,0:T(8,128)(2,1)} %pad_maximum_fusion.5.refs_0_, bf16[4,48,1536]{2,1,0:T(8,128)(2,1)} %collective-permute-done.24.refs_1_, bf16[4,48,1536]{2,1,0:T(8,128)(2,1)} %collective-permute-done.25.refs_2_, ...), custom_call_target="tpu_custom_call" | custom-call | bytes 9437184 | tf_op jit(solution)/shard_map/assemble/pallas_call | solution.py:102
  130.7 6.3 %assemble.4 = (bf16[768,1920]{1,0:T(8,128)(2,1)}, bf16[768,1920]{1,0:T(8,128)(2,1)}) custom-call(s32[3]{0:T(128)} %pad_add_fusion.1.where, bf16[4,48,1920]{2,1,0:T(8,128)(2,1)} %pad_maximum_fusion.4.refs_0_, bf16[4,48,1920]{2,1,0:T(8,128)(2,1)} %collective-permute-done.13.refs_1_, bf16[4,48,1920]{2,1,0:T(8,128)(2,1)} %copy-done.21, ...), custom_call_target="tpu_custom_call" | custom-call | bytes 11796480 | tf_op jit(solution)/shard_map/assemble/pallas_call | solution.py:102
  170.6 5.8 %fusion.100 = (bf16[1536]{0:T(1024)(128)(2,1)S(1)}, bf16[1024,1536]{1,0:T(8,128)(2,1)S(1)}) fusion(f32[1024,1536]{1,0:T(8,128)S(1)} %get-tuple-element.185, f32[1536]{0:T(1024)S(1)} %add.312, bf16[1024,768]{0,1:T(8,128)(2,1)S(1)} %get-tuple-element.145, bf16[768,1536]{1,0:T(8,128)(2,1)S(1)} %copy-done.32), kind=kOutput, calls=%fused_computation.241 | convolution fusion | flops 2437937664 | bytes 13378560 | tf_op jit(solution)/shard_map/dot_general | solution.py:25
  184.8 6.4 %fusion.99 = (bf16[1536]{0:T(1024)(128)(2,1)}, bf16[1024,1536]{1,0:T(8,128)(2,1)S(1)}) fusion(f32[1024,1536]{1,0:T(8,128)S(1)} %get-tuple-element.187, f32[1536]{0:T(1024)S(1)} %add.308, bf16[1024,768]{0,1:T(8,128)(2,1)S(1)} %get-tuple-element.145, bf16[768,1536]{1,0:T(8,128)(2,1)S(1)} %copy-done.31), kind=kOutput, calls=%fused_computation.240 | convolution fusion | flops 2437937664 | bytes 13378560 | tf_op jit(solution)/shard_map/dot_general | solution.py:25
  196.9 6.1 %multiply_reduce_fusion = (bf16[768]{0:T(1024)(128)(2,1)S(1)}, f32[1024]{0:T(1024)S(1)}, f32[1024]{0:T(1024)S(1)}, bf16[768]{0:T(1024)(128)(2,1)S(1)}, f32[1024,768]{0,1:T(8,128)S(1)}) fusion(f32[1024,768]{0,1:T(8,128)S(1)} %get-tuple-element.183, f32[1024]{0:T(1024)S(1)} %add_rsqrt_fusion.1, f32[1024]{0:T(1024)S(1)} %broadcast_multiply_fusion.5, ...), kind=kOutput, calls=%fused_computation.35 | convolution fusion | flops 2430857728 | bytes 19704832 | tf_op jit(solution)/shard_map/dot_general | solution.py:25
  212.8 11.0 %attn_bwd.3 = (bf16[1024,384]{1,0:T(8,128)(2,1)}, bf16[1024,384]{1,0:T(8,128)(2,1)}, bf16[1024,384]{1,0:T(8,128)(2,1)}) custom-call(s32[24]{0:T(128)} %copy-done.29, bf16[1024,1152]{1,0:T(8,128)(2,1)} %add_convert_fusion.q_ref.k_ref.v_ref, bf16[1024,1152]{1,0:T(8,128)(2,1)} %add_convert_fusion.q_ref.k_ref.v_ref, ...), custom_call_target="tpu_custom_call" | custom-call | flops 2415919104 | bytes 10616832 | tf_op jit(solution)/shard_map/attn_bwd/pallas_call | solution.py:333
  233.6 11.0 %attn_bwd.2 = (bf16[1024,384]{1,0:T(8,128)(2,1)}, bf16[1024,384]{1,0:T(8,128)(2,1)}, bf16[1024,384]{1,0:T(8,128)(2,1)}) custom-call(s32[24]{0:T(128)} %get-tuple-element.178.table, bf16[1024,1152]{1,0:T(8,128)(2,1)} %add_convert_fusion.1.q_ref.k_ref.v_ref, bf16[1024,1152]{1,0:T(8,128)(2,1)} %add_convert_fusion.1.q_ref.k_ref.v_ref, ...), custom_call_target="tpu_custom_call" | custom-call | flops 2415919104 | bytes 10616832 | tf_op jit(solution)/shard_map/attn_bwd/pallas_call | solution.py:333
  252.6 5.6 %convolution_convert_fusion.5 = bf16[768,1152]{1,0:T(8,128)(2,1)} fusion(bf16[1024,768]{1,0:T(8,128)(2,1)} %constant_dynamic-slice_fusion.3, bf16[1024,1152]{1,0:T(8,128)(2,1)} %constant_dynamic-update-slice_fusion), kind=kOutput, calls=%fused_computation.30 | convolution fusion | flops 1812824064 | bytes 5701632 | tf_op jit(solution)/shard_map/dot_general | solution.py:25
  258.2 5.5 %split.5 = (bf16[2,2,4,48,1536]{4,3,2,1,0:T(8,128)(2,1)}, bf16[2,2,4,48,1536]{4,3,2,1,0:T(8,128)(2,1)}) custom-call(s32[3]{0:T(128)} %pad_add_fusion.1.where, bf16[768,1536]{1,0:T(8,128)(2,1)} %convolution_convert_fusion.1.own_ref, bf16[768,1536]{1,0:T(8,128)(2,1)} %convolution_convert_fusion.other_ref), custom_call_target="tpu_custom_call" | custom-call | bytes 9437184 | tf_op jit(solution)/shard_map/split/pallas_call | solution.py:157
  285.7 6.2 %split.4 = (bf16[2,2,4,48,1920]{4,3,2,1,0:T(8,128)(2,1)}, bf16[2,2,4,48,1920]{4,3,2,1,0:T(8,128)(2,1)}) custom-call(s32[3]{0:T(128)} %pad_add_fusion.1.where, bf16[768,1920]{1,0:T(8,128)(2,1)} %pad_maximum_fusion.own_ref, bf16[768,1920]{1,0:T(8,128)(2,1)} %pad_maximum_fusion.1.other_ref), custom_call_target="tpu_custom_call" | custom-call | bytes 11796480 | tf_op jit(solution)/shard_map/split/pallas_call | solution.py:157
  296.6 6.2 %fusion.98 = (bf16[1024,768]{0,1:T(8,128)(2,1)}, f32[1024,768]{0,1:T(8,128)}) fusion(f32[1024,768]{0,1:T(8,128)S(1)} %get-tuple-element.142, f32[1024,768]{0,1:T(8,128)S(1)} %fusion.26, bf16[1024,1152]{1,0:T(8,128)(2,1)} %constant_dynamic-update-slice_fusion, bf16[768,1280]{1,0:T(8,128)(2,1)S(1)} %copy-done.27), kind=kOutput, calls=%fused_computation.239 | convolution fusion | flops 1814298624 | bytes 15138816 | tf_op jit(solution)/shard_map/dot_general | solution.py:25
  319.4 20.9 %collective-permute-done.32 = bf16[1024,768]{0,1:T(8,128)(2,1)} collective-permute-done((bf16[1024,768]{0,1:T(8,128)(2,1)}, bf16[1024,768]{0,1:T(8,128)(2,1)}, u32[]{:S(2)}, u32[]{:S(2)}) %collective-permute-start.32) | collective-permute-done | bytes 1572896 | tf_op jit(solution)/shard_map/ppermute | solution.py:50
  342.1 31.4 %collective-permute-done.31 = bf16[1024,768]{0,1:T(8,128)(2,1)} collective-permute-done((bf16[1024,768]{0,1:T(8,128)(2,1)}, bf16[1024,768]{0,1:T(8,128)(2,1)}, u32[]{:S(2)}, u32[]{:S(2)}) %collective-permute-start.31) | collective-permute-done | bytes 1572896 | tf_op jit(solution)/shard_map/ppermute | solution.py:50
  388.6 8.0 %collective-permute-done.35 = bf16[4,48,1280]{2,1,0:T(8,128)(2,1)S(1)} collective-permute-done((bf16[4,48,1280]{2,1,0:T(8,128)(2,1)S(1)}, bf16[4,48,1280]{2,1,0:T(8,128)(2,1)S(1)}, u32[]{:S(2)}, u32[]{:S(2)}) %collective-permute-start.35) | collective-permute-done | bytes 491552 | tf_op jit(solution)/shard_map/ppermute | solution.py:46
  401.7 8.7 %collective-permute-done.46 = bf16[2,4,48,1536]{3,2,1,0:T(8,128)(2,1)S(1)} collective-permute-done((bf16[2,4,48,1536]{3,2,1,0:T(8,128)(2,1)S(1)}, bf16[2,4,48,1536]{3,2,1,0:T(8,128)(2,1)S(1)}, u32[]{:S(2)}, u32[]{:S(2)}) %collective-permute-start.46) | collective-permute-done | bytes 1179680 | tf_op jit(solution)/shard_map/ppermute | solution.py:46
  412.9 27.7 %collective-permute-done.40 = bf16[2,4,48,1920]{3,2,1,0:T(8,128)(2,1)S(1)} collective-permute-done((bf16[2,4,48,1920]{3,2,1,0:T(8,128)(2,1)S(1)}, bf16[2,4,48,1920]{3,2,1,0:T(8,128)(2,1)S(1)}, u32[]{:S(2)}, u32[]{:S(2)}) %collective-permute-start.40) | collective-permute-done | bytes 1474592 | tf_op jit(solution)/shard_map/ppermute | solution.py:46
  452.5 7.0 %collective-permute-done.41 = bf16[4,48,1920]{2,1,0:T(8,128)(2,1)} collective-permute-done((bf16[4,48,1920]{2,1,0:T(8,128)(2,1)}, bf16[4,48,1920]{2,1,0:T(8,128)(2,1)}, u32[]{:S(2)}, u32[]{:S(2)}) %collective-permute-start.41) | collective-permute-done | bytes 737312 | tf_op jit(solution)/shard_map/ppermute | solution.py:46
  (314 shorter events, 237.6 us)
Async XLA Ops:
  39.2 20.0 %collective-permute-start.6 = (bf16[4,48,1280]{2,1,0:T(8,128)(2,1)}, bf16[4,48,1280]{2,1,0:T(8,128)(2,1)}, u32[]{:S(2)}, u32[]{:S(2)}) collective-permute-start(bf16[4,48,1280]{2,1,0:T(8,128)(2,1)} %pad_maximum_fusion.6.refs_0_), channel_id=1, source_target_pairs={{0,2},{1,3},{2,0},{3,1},{4,6},{5,7},{6,4},{7,5},{8,10},{9,11},{10,... | collective-permute-start | bytes 1474568 | tf_op jit(solution)/shard_map/ppermute | solution.py:46
  59.2 32.2 %collective-permute-start.24 = (bf16[4,48,1536]{2,1,0:T(8,128)(2,1)}, bf16[4,48,1536]{2,1,0:T(8,128)(2,1)}, u32[]{:S(2)}, u32[]{:S(2)}) collective-permute-start(bf16[4,48,1536]{2,1,0:T(8,128)(2,1)} %pad_maximum_fusion.5.refs_0_), channel_id=1, source_target_pairs={{0,1},{1,0},{2,6},{3,7},{4,5},{5,4},{6,2},{7,3},{8,9},{9,8},{10,14... | collective-permute-start | bytes 1769480 | tf_op jit(solution)/shard_map/ppermute | solution.py:46
  59.8 32.5 %collective-permute-start.25 = (bf16[4,48,1536]{2,1,0:T(8,128)(2,1)}, bf16[4,48,1536]{2,1,0:T(8,128)(2,1)}, u32[]{:S(2)}, u32[]{:S(2)}) collective-permute-start(bf16[4,48,1536]{2,1,0:T(8,128)(2,1)} %pad_maximum_fusion.5.refs_0_), channel_id=1, source_target_pairs={{0,4},{1,5},{2,3},{3,2},{4,0},{5,1},{6,7},{7,6},{8,12},{9,13},{10,... | collective-permute-start | bytes 1769480 | tf_op jit(solution)/shard_map/ppermute | solution.py:46
  60.3 32.1 %collective-permute-start.27 = (bf16[4,48,1536]{2,1,0:T(8,128)(2,1)}, bf16[4,48,1536]{2,1,0:T(8,128)(2,1)}, u32[]{:S(2)}, u32[]{:S(2)}) collective-permute-start(bf16[4,48,1536]{2,1,0:T(8,128)(2,1)} %pad_maximum_fusion.5.refs_0_), channel_id=1, source_target_pairs={{0,2},{1,3},{2,0},{3,1},{4,6},{5,7},{6,4},{7,5},{8,10},{9,11},{10,... | collective-permute-start | bytes 1769480 | tf_op jit(solution)/shard_map/ppermute | solution.py:46
  60.3 30.0 %collective-permute-start.13 = (bf16[4,48,1920]{2,1,0:T(8,128)(2,1)}, bf16[4,48,1920]{2,1,0:T(8,128)(2,1)}, u32[]{:S(2)}, u32[]{:S(2)}) collective-permute-start(bf16[4,48,1920]{2,1,0:T(8,128)(2,1)} %pad_maximum_fusion.4.refs_0_), channel_id=1, source_target_pairs={{0,1},{1,0},{2,6},{3,7},{4,5},{5,4},{6,2},{7,3},{8,9},{9,8},{10,14... | collective-permute-start | bytes 2211848 | tf_op jit(solution)/shard_map/ppermute | solution.py:46
  70.4 37.3 %collective-permute-start.14 = (bf16[4,48,1920]{2,1,0:T(8,128)(2,1)}, bf16[4,48,1920]{2,1,0:T(8,128)(2,1)S(1)}, u32[]{:S(2)}, u32[]{:S(2)}) collective-permute-start(bf16[4,48,1920]{2,1,0:T(8,128)(2,1)} %pad_maximum_fusion.4.refs_0_), channel_id=1, source_target_pairs={{0,4},{1,5},{2,3},{3,2},{4,0},{5,1},{6,7},{7,6},{8,12},{9,13},{10,... | collective-permute-start | bytes 2211848 | tf_op jit(solution)/shard_map/ppermute | solution.py:46
  90.2 18.7 %collective-permute-start.15 = (bf16[4,48,1920]{2,1,0:T(8,128)(2,1)}, bf16[4,48,1920]{2,1,0:T(8,128)(2,1)}, u32[]{:S(2)}, u32[]{:S(2)}) collective-permute-start(bf16[4,48,1920]{2,1,0:T(8,128)(2,1)} %collective-permute-done.13.refs_1_), channel_id=1, source_target_pairs={{0,4},{1,5},{2,3},{3,2},{4,0},{5,1},{6,7},{7,6},{8,12},{9,13},{10,... | collective-permute-start | bytes 2211848 | tf_op jit(solution)/shard_map/ppermute | solution.py:46
  91.4 16.9 %collective-permute-start.26 = (bf16[4,48,1536]{2,1,0:T(8,128)(2,1)}, bf16[4,48,1536]{2,1,0:T(8,128)(2,1)}, u32[]{:S(2)}, u32[]{:S(2)}) collective-permute-start(bf16[4,48,1536]{2,1,0:T(8,128)(2,1)} %collective-permute-done.24.refs_1_), channel_id=1, source_target_pairs={{0,4},{1,5},{2,3},{3,2},{4,0},{5,1},{6,7},{7,6},{8,12},{9,13},{10,... | collective-permute-start | bytes 1769480 | tf_op jit(solution)/shard_map/ppermute | solution.py:46
  107.7 23.0 %collective-permute-start.16 = (bf16[4,48,1920]{2,1,0:T(8,128)(2,1)}, bf16[4,48,1920]{2,1,0:T(8,128)(2,1)}, u32[]{:S(2)}, u32[]{:S(2)}) collective-permute-start(bf16[4,48,1920]{2,1,0:T(8,128)(2,1)} %pad_maximum_fusion.4.refs_0_), channel_id=1, source_target_pairs={{0,2},{1,3},{2,0},{3,1},{4,6},{5,7},{6,4},{7,5},{8,10},{9,11},{10,... | collective-permute-start | bytes 2211848 | tf_op jit(solution)/shard_map/ppermute | solution.py:46
  108.3 22.3 %collective-permute-start.17 = (bf16[4,48,1920]{2,1,0:T(8,128)(2,1)}, bf16[4,48,1920]{2,1,0:T(8,128)(2,1)}, u32[]{:S(2)}, u32[]{:S(2)}) collective-permute-start(bf16[4,48,1920]{2,1,0:T(8,128)(2,1)} %collective-permute-done.13.refs_1_), channel_id=1, source_target_pairs={{0,2},{1,3},{2,0},{3,1},{4,6},{5,7},{6,4},{7,5},{8,10},{9,11},{10,... | collective-permute-start | bytes 2211848 | tf_op jit(solution)/shard_map/ppermute | solution.py:46
  108.4 22.4 %collective-permute-start.18 = (bf16[4,48,1920]{2,1,0:T(8,128)(2,1)S(1)}, bf16[4,48,1920]{2,1,0:T(8,128)(2,1)}, u32[]{:S(2)}, u32[]{:S(2)}) collective-permute-start(bf16[4,48,1920]{2,1,0:T(8,128)(2,1)S(1)} %collective-permute-done.14.refs_2_), channel_id=1, source_target_pairs={{0,2},{1,3},{2,0},{3,1},{4,6},{5,7},{6,4},{7,5},{8,10},{9,11},{10,... | collective-permute-start | bytes 2211848 | tf_op jit(solution)/shard_map/ppermute | solution.py:46
  108.9 21.8 %collective-permute-start.19 = (bf16[4,48,1920]{2,1,0:T(8,128)(2,1)}, bf16[4,48,1920]{2,1,0:T(8,128)(2,1)}, u32[]{:S(2)}, u32[]{:S(2)}) collective-permute-start(bf16[4,48,1920]{2,1,0:T(8,128)(2,1)} %collective-permute-done.15.refs_3_), channel_id=1, source_target_pairs={{0,2},{1,3},{2,0},{3,1},{4,6},{5,7},{6,4},{7,5},{8,10},{9,11},{10,... | collective-permute-start | bytes 2211848 | tf_op jit(solution)/shard_map/ppermute | solution.py:46
  263.7 114.6 %collective-permute-start.45 = (bf16[2,2,4,48,1536]{4,3,2,1,0:T(8,128)(2,1)}, bf16[2,2,4,48,1536]{4,3,2,1,0:T(8,128)(2,1)}, u32[]{:S(2)}, u32[]{:S(2)}) collective-permute-start(bf16[2,2,4,48,1536]{4,3,2,1,0:T(8,128)(2,1)} %get-tuple-element.57), channel_id=1, source_target_pairs={{0,2},{1,3},{2,0},{3,1},{4,6},{5,7},{6,4},{7,5},{8,10},{9,11},{10,... | collective-permute-start | bytes 7077896 | tf_op jit(solution)/shard_map/ppermute | solution.py:46
  279.5 27.1 %collective-permute-start.33 = (bf16[2,2,4,48,1280]{4,3,2,1,0:T(8,128)(2,1)}, bf16[2,2,4,48,1280]{4,3,2,1,0:T(8,128)(2,1)}, u32[]{:S(2)}, u32[]{:S(2)}) collective-permute-start(bf16[2,2,4,48,1280]{4,3,2,1,0:T(8,128)(2,1)} %get-tuple-element.53), channel_id=1, source_target_pairs={{0,2},{1,3},{2,0},{3,1},{4,6},{5,7},{6,4},{7,5},{8,10},{9,11},{10,... | collective-permute-start | bytes 5898248 | tf_op jit(solution)/shard_map/ppermute | solution.py:46
  292.0 93.1 %collective-permute-start.39 = (bf16[2,2,4,48,1920]{4,3,2,1,0:T(8,128)(2,1)}, bf16[2,2,4,48,1920]{4,3,2,1,0:T(8,128)(2,1)}, u32[]{:S(2)}, u32[]{:S(2)}) collective-permute-start(bf16[2,2,4,48,1920]{4,3,2,1,0:T(8,128)(2,1)} %get-tuple-element.55), channel_id=1, source_target_pairs={{0,2},{1,3},{2,0},{3,1},{4,6},{5,7},{6,4},{7,5},{8,10},{9,11},{10,... | collective-permute-start | bytes 8847368 | tf_op jit(solution)/shard_map/ppermute | solution.py:46
  302.8 37.6 %collective-permute-start.32 = (bf16[1024,768]{0,1:T(8,128)(2,1)}, bf16[1024,768]{0,1:T(8,128)(2,1)}, u32[]{:S(2)}, u32[]{:S(2)}) collective-permute-start(bf16[1024,768]{0,1:T(8,128)(2,1)} %get-tuple-element.191), channel_id=1, source_target_pairs={{0,1},{1,0},{2,3},{3,2},{4,5},{5,4},{6,7},{7,6},{8,9},{9,8},{10,11... | collective-permute-start | bytes 4718600 | tf_op jit(solution)/shard_map/ppermute | solution.py:50
  302.8 70.7 %collective-permute-start.31 = (bf16[1024,768]{0,1:T(8,128)(2,1)}, bf16[1024,768]{0,1:T(8,128)(2,1)}, u32[]{:S(2)}, u32[]{:S(2)}) collective-permute-start(bf16[1024,768]{0,1:T(8,128)(2,1)} %get-tuple-element.150), channel_id=1, source_target_pairs={{0,1},{1,0},{2,3},{3,2},{4,5},{5,4},{6,7},{7,6},{8,9},{9,8},{10,11... | collective-permute-start | bytes 4718600 | tf_op jit(solution)/shard_map/ppermute | solution.py:50
  310.4 72.3 %collective-permute-start.34 = (bf16[2,4,48,1280]{3,2,1,0:T(8,128)(2,1)}, bf16[2,4,48,1280]{3,2,1,0:T(8,128)(2,1)}, u32[]{:S(2)}, u32[]{:S(2)}) collective-permute-start(bf16[2,4,48,1280]{3,2,1,0:T(8,128)(2,1)} %get-tuple-element.149), channel_id=1, source_target_pairs={{0,4},{1,5},{2,6},{3,7},{4,0},{5,1},{6,2},{7,3},{8,12},{9,13},{10,... | collective-permute-start | bytes 2949128 | tf_op jit(solution)/shard_map/ppermute | solution.py:46
  381.5 28.9 %collective-permute-start.46 = (bf16[2,4,48,1536]{3,2,1,0:T(8,128)(2,1)S(1)}, bf16[2,4,48,1536]{3,2,1,0:T(8,128)(2,1)S(1)}, u32[]{:S(2)}, u32[]{:S(2)}) collective-permute-start(bf16[2,4,48,1536]{3,2,1,0:T(8,128)(2,1)S(1)} %get-tuple-element.147), channel_id=1, source_target_pairs={{0,4},{1,5},{2,6},{3,7},{4,0},{5,1},{6,2},{7,3},{8,12},{9,13},{10,... | collective-permute-start | bytes 3538952 | tf_op jit(solution)/shard_map/ppermute | solution.py:46
  387.8 52.8 %collective-permute-start.40 = (bf16[2,4,48,1920]{3,2,1,0:T(8,128)(2,1)S(1)}, bf16[2,4,48,1920]{3,2,1,0:T(8,128)(2,1)S(1)}, u32[]{:S(2)}, u32[]{:S(2)}) collective-permute-start(bf16[2,4,48,1920]{3,2,1,0:T(8,128)(2,1)S(1)} %get-tuple-element.144), channel_id=1, source_target_pairs={{0,4},{1,5},{2,6},{3,7},{4,0},{5,1},{6,2},{7,3},{8,12},{9,13},{10,... | collective-permute-start | bytes 4423688 | tf_op jit(solution)/shard_map/ppermute | solution.py:46
  411.8 33.1 %collective-permute-start.47 = (bf16[4,48,1536]{2,1,0:T(8,128)(2,1)}, bf16[4,48,1536]{2,1,0:T(8,128)(2,1)}, u32[]{:S(2)}, u32[]{:S(2)}) collective-permute-start(bf16[4,48,1536]{2,1,0:T(8,128)(2,1)} %get-tuple-element.154), channel_id=1, source_target_pairs={{0,1},{1,0},{2,3},{3,2},{4,5},{5,4},{6,7},{7,6},{8,9},{9,8},{10,11... | collective-permute-start | bytes 1769480 | tf_op jit(solution)/shard_map/ppermute | solution.py:46
  442.1 17.4 %collective-permute-start.41 = (bf16[4,48,1920]{2,1,0:T(8,128)(2,1)}, bf16[4,48,1920]{2,1,0:T(8,128)(2,1)}, u32[]{:S(2)}, u32[]{:S(2)}) collective-permute-start(bf16[4,48,1920]{2,1,0:T(8,128)(2,1)} %get-tuple-element.152), channel_id=1, source_target_pairs={{0,1},{1,0},{2,3},{3,2},{4,5},{5,4},{6,7},{7,6},{8,9},{9,8},{10,11... | collective-permute-start | bytes 2211848 | tf_op jit(solution)/shard_map/ppermute | solution.py:46
  446.2 18.4 %collective-permute-start.48 = (bf16[48,1536]{1,0:T(8,128)(2,1)S(1)}, bf16[48,1536]{1,0:T(8,128)(2,1)S(1)}, u32[]{:S(2)}, u32[]{:S(2)}) collective-permute-start(bf16[48,1536]{1,0:T(8,128)(2,1)S(1)} %get-tuple-element.162), channel_id=1, source_target_pairs={{0,8},{1,9},{2,10},{3,11},{4,12},{5,13},{6,14},{7,15},{8,16},{9,17... | collective-permute-start | bytes 442376 | tf_op jit(solution)/shard_map/ppermute | solution.py:46
  448.4 18.2 %collective-permute-start.49 = (bf16[48,1536]{1,0:T(8,128)(2,1)S(1)}, bf16[48,1536]{1,0:T(8,128)(2,1)S(1)}, u32[]{:S(2)}, u32[]{:S(2)}) collective-permute-start(bf16[48,1536]{1,0:T(8,128)(2,1)S(1)} %get-tuple-element.164), channel_id=1, source_target_pairs={{0,16},{1,17},{2,18},{3,19},{4,20},{5,21},{6,22},{7,23},{8,24},{9,... | collective-permute-start | bytes 442376 | tf_op jit(solution)/shard_map/ppermute | solution.py:46
  (64 other events, 633.5 us)

commit v2 on v1

v2 whole, which is shorter than its diff:
```python
import functools

import jax
import jax.numpy as jnp
from jax import lax
from jax.experimental import pallas as pl
from jax.experimental.pallas import tpu as pltpu
from jax.sharding import PartitionSpec as P

HD = 64
PAIR = 2 * HD
BLOCK = 256
HALF = 2 * BLOCK
NORM_EPS = 1e-05
BF = jnp.bfloat16
F32 = jnp.float32
AXES = ("dp", "mp")
NN = (((1,), (0,)), ((), ()))
NT = (((1,), (1,)), ((), ()))
TN = (((0,), (0,)), ((), ()))
SMALL = 128


def mm(first, second, dims):
    return lax.dot_general(first, second, dims, preferred_element_type=F32)


def pairs_of(step):
    moves = []
    for d in range(16):
        for m in range(2):
            d2, m2 = step(d, m)
            moves.append((2 * d + m, 2 * d2 + m2))
    return moves


MOVE_X = pairs_of(lambda d, m: (d, 1 - m))
MOVE_Y = pairs_of(lambda d, m: (d ^ 2, m))
MOVE_CORE = pairs_of(lambda d, m: (d ^ 1, m))
MOVE_Z = [pairs_of(lambda d, m, k=k: ((d + 4 * k) % 16, m)) for k in (1, 2, 3)]
MOVE_FIRST = pairs_of(lambda d, m: (d ^ 2, m) if d & 1 else (d, 1 - m))
MOVE_SECOND = pairs_of(lambda d, m: (d, 1 - m) if d & 1 else (d ^ 2, m))


MOVE_REDUCE = MOVE_SECOND, MOVE_FIRST


def move(values, moves):
    return lax.ppermute(values, AXES, moves)


def swap_mp(values):
    return lax.ppermute(values, "mp", [(0, 1), (1, 0)])


def piece_copies(where, pieces, target, sem):
    if len(pieces) == 2:
        waits = [pltpu.make_async_copy(p, target.at[n], sem.at[n, 0]) for n, p in enumerate(pieces)]
        for copy in waits:
            copy.start()
        return waits
    rows = pieces[0].shape[1]
    z, y, core = where[0], where[1], where[2]
    z0, a0, b0, c0, z1, a1, b1, c1 = pieces
    first = core == 0

    def copies(ref, half, dy, dcore, slot):
        out = []
        for k in range(4):
            block = ((lax.rem(z + 4 - k, 4) * 2 + (y ^ dy)) * 2 + (core ^ dcore)) * rows
            block = pl.multiple_of(block, 16)
            out.append(
                pltpu.make_async_copy(
                    ref.at[k], target.at[half, pl.ds(block, rows), :], sem.at[slot, k]
                )
            )
        return out

    waits = []
    for slot, (ref, half, dy, dcore) in enumerate(
        ((z0, 0, 0, 0), (c0, 1, 1, 0), (z1, 0, 0, 1), (c1, 1, 1, 1))
    ):
        waits += copies(ref, half, dy, dcore, slot)
    for copy in waits:
        copy.start()
    for slot, (ref_if, ref_else, half, dy, dcore) in enumerate(
        ((b0, a0, 0, 1, 0), (a0, b0, 1, 0, 0), (a1, b1, 0, 1, 1), (b1, a1, 1, 0, 1)), 4
    ):
        @pl.when(first)
        def _(ref=ref_if, half=half, dy=dy, dcore=dcore, slot=slot):
            for copy in copies(ref, half, dy, dcore, slot):
                copy.start()

        @pl.when(jnp.logical_not(first))
        def _(ref=ref_else, half=half, dy=dy, dcore=dcore, slot=slot):
            for copy in copies(ref, half, dy, dcore, slot):
                copy.start()

        waits += copies(ref_if, half, dy, dcore, slot)
    return waits


def assemble_kernel(count, where, *refs):
    pieces, (own_ref, other_ref, target, sem) = refs[:count], refs[count:]
    for copy in piece_copies(where, pieces, target, sem):
        copy.wait()
    own_ref[...] = target[0]
    other_ref[...] = target[1]


def assemble(where, pieces):
    rows, cols = pieces[0].shape[1:]
    full = jax.ShapeDtypeStruct((16 * rows, cols), pieces[0].dtype)
    return pl.pallas_call(
        functools.partial(assemble_kernel, len(pieces)),
        out_shape=(full, full),
        grid_spec=pltpu.PrefetchScalarGridSpec(
            num_scalar_prefetch=1,
            grid=(1,),
            in_specs=[pl.BlockSpec(memory_space=pl.ANY)] * len(pieces),
            out_specs=[pl.BlockSpec((16 * rows, cols), lambda i, w: (0, 0))] * 2,
            scratch_shapes=[
                pltpu.VMEM((2, 16 * rows, cols), BF),
                pltpu.SemaphoreType.DMA((8, 4)),
            ],
        ),
        cost_estimate=pl.CostEstimate(
            flops=0, transcendentals=0, bytes_accessed=64 * rows * cols * 2
        ),
        name="assemble",
    )(where, *pieces)


def part_copies(where, result, half, keep_ref, send_ref, sem, staged):
    if not staged:
        return [pltpu.make_async_copy(result.at[half], keep_ref.at[half], sem.at[half, 0])]
    rows = keep_ref.shape[-2]
    z, y, core = where[0], where[1], where[2]
    out = []
    for dcore, target in enumerate((keep_ref, send_ref)):
        for dy in range(2):
            for k in range(4):
                block = ((lax.rem(z + k, 4) * 2 + (y ^ dy)) * 2 + (core ^ dcore)) * rows
                block = pl.multiple_of(block, 16)
                if target.shape[2] == 1:
                    place = target.at[dy, k, 0]
                else:
                    by_y = (core ^ dcore) == 0
                    place = target.at[jnp.where(by_y, dy, half), jnp.where(by_y, half, dy), k]
                out.append(
                    pltpu.make_async_copy(
                        result.at[half, pl.ds(block, rows), :], place, sem.at[half, len(out)]
                    )
                )
    return out


def part_shapes(staged, halves, d_model, cols):
    if not staged:
        whole = jax.ShapeDtypeStruct((halves, d_model, cols), BF)
        return whole, jax.ShapeDtypeStruct((8, 128), BF)
    rows = d_model // 16
    dims = (2, 4, 1, rows, cols) if halves == 1 else (2, 2, 4, rows, cols)
    return (jax.ShapeDtypeStruct(dims, BF),) * 2


def after(value, *others):
    return lax.optimization_barrier((value, *others))[0]


def grads_kernel(staged, halves, widths, where, *refs):
    count = len(widths)
    lhs_refs, refs = refs[:count], refs[count:]
    rhs_refs, refs = refs[: count * halves], refs[count * halves :]
    extra_ref, keep_ref, send_ref, result, turned, sem = refs
    for lhs, out in zip(lhs_refs, range(count)):
        for at in range(0, lhs.shape[0], BLOCK):
            turned[out, :, at : at + BLOCK] = lhs[at : at + BLOCK, :].T
    for half in range(halves):
        first = 0
        for n in range(count):
            rhs = rhs_refs[n * halves + half]
            rhs = rhs.at[half] if len(rhs.shape) == 3 else rhs
            width = rhs.shape[1]
            for at in range(0, width, 384):
                result[half, :, first + at : first + at + 384] = mm(
                    turned[n], rhs[:, at : at + 384], NN
                ).astype(BF)
            first += width
        result[half, :, first:] = extra_ref[half]
        for copy in part_copies(where, result, half, keep_ref, send_ref, sem, staged):
            copy.start()
    for half in range(halves):
        for copy in part_copies(where, result, half, keep_ref, send_ref, sem, staged):
            copy.wait()


def whole_spec(array):
    return pl.BlockSpec(array.shape, lambda i, w, n=array.ndim: (0,) * n)


def grads(where, staged, lhs, rhs, extra):
    seq, d_model = lhs[0].shape
    halves = extra.shape[0]
    widths = [r[0].shape[-1] for r in rhs]
    cols = sum(widths) + extra.shape[2]
    operands = [*lhs, *(r for pair in rhs for r in pair), extra]
    return pl.pallas_call(
        functools.partial(grads_kernel, staged, halves, widths),
        out_shape=part_shapes(staged, halves, d_model, cols),
        grid_spec=pltpu.PrefetchScalarGridSpec(
            num_scalar_prefetch=1,
            grid=(1,),
            in_specs=[whole_spec(o) for o in operands],
            out_specs=[pl.BlockSpec(memory_space=pl.ANY)] * 2,
            scratch_shapes=[
                pltpu.VMEM((halves, d_model, cols), BF),
                pltpu.VMEM((len(lhs), d_model, seq), BF),
                pltpu.SemaphoreType.DMA((halves, 16)),
            ],
        ),
        cost_estimate=pl.CostEstimate(
            flops=2 * seq * d_model * halves * sum(widths),
            transcendentals=0,
            bytes_accessed=halves * (seq + d_model) * cols * 2,
        ),
        name="grads",
    )(where, *operands)


def row_norm(values):
    centered = values - jnp.mean(values, axis=-1, keepdims=True)
    inverse = lax.rsqrt(jnp.mean(centered * centered, axis=-1, keepdims=True) + NORM_EPS)
    return centered * inverse, inverse


def row_norm_back(d_normed, z, inverse, gain):
    dz = d_normed * gain
    return (
        dz - jnp.mean(dz, axis=-1, keepdims=True) - z * jnp.mean(dz * z, axis=-1, keepdims=True)
    ) * inverse


def column_sum(values):
    return jnp.sum(values, axis=0, keepdims=True)


def first_kernel(n_up, where, tok_ref, ctx0_ref, ctx1_ref, vec_ref, bias_ref, *refs):
    pieces = refs[:n_up]
    z_ref, inv_ref, hid_ref, slope_ref, weights, sem = refs[n_up:]
    width = ctx0_ref.shape[1]

    @pl.when(pl.program_id(0) == 0)
    def _():
        for copy in piece_copies(where, pieces, weights, sem):
            copy.wait()

    resid = (
        tok_ref[...].astype(F32)
        + mm(ctx0_ref[...], weights[0, :, :width], NT)
        + mm(ctx1_ref[...], weights[1, :, :width], NT)
        + vec_ref[0:1]
    )
    z, inverse = row_norm(resid)
    z_ref[...] = z
    inv_ref[...] = jnp.broadcast_to(inverse, inv_ref.shape)
    low = (z * vec_ref[1:2] + vec_ref[2:3]).astype(BF)
    ff = hid_ref.shape[2]
    for half in range(2):
        for at in range(0, ff, 512):
            pre = mm(low, weights[half, :, width + at : width + at + 512], NN)
            gelu, slope = gelu_both(pre + bias_ref[half, :, at : at + 512])
            hid_ref[half, :, at : at + 512] = gelu.astype(BF)
            slope_ref[half, :, at : at + 512] = slope.astype(BF)


def row_tile(tile, width):
    return pl.BlockSpec((tile, width), lambda i, w: (i, 0))


def halves_tile(tile, width):
    return pl.BlockSpec((2, tile, width), lambda i, w: (0, i, 0))


ANYWHERE = pl.BlockSpec(memory_space=pl.ANY)


def first_part(where, tokens, ctx, vectors, bias, pieces, tile=256):
    seq, d_model = tokens.shape
    width, ff = ctx[0].shape[1], bias.shape[2]
    return pl.pallas_call(
        functools.partial(first_kernel, len(pieces)),
        out_shape=(
            jax.ShapeDtypeStruct((seq, d_model), F32),
            jax.ShapeDtypeStruct((seq, 128), F32),
            jax.ShapeDtypeStruct((2, seq, ff), BF),
            jax.ShapeDtypeStruct((2, seq, ff), BF),
        ),
        grid_spec=pltpu.PrefetchScalarGridSpec(
            num_scalar_prefetch=1,
            grid=(seq // tile,),
            in_specs=[
                row_tile(tile, d_model),
                row_tile(tile, width),
                row_tile(tile, width),
                whole_spec(vectors),
                whole_spec(bias),
            ]
            + [ANYWHERE] * len(pieces),
            out_specs=[
                row_tile(tile, d_model),
                row_tile(tile, 128),
                halves_tile(tile, ff),
                halves_tile(tile, ff),
            ],
            scratch_shapes=[
                pltpu.VMEM((2, d_model, width + ff), BF),
                pltpu.SemaphoreType.DMA((8, 4)),
            ],
        ),
        cost_estimate=pl.CostEstimate(
            flops=2 * seq * d_model * 2 * (width + ff),
            transcendentals=seq * 2 * ff * 2,
            bytes_accessed=seq * (d_model * 8 + ff * 8) + d_model * 4 * (width + ff),
        ),
        name="first_part",
    )(where, tokens, *ctx, vectors, bias, *pieces)


def second_kernel(staged, n_down, where, hid_ref, z_ref, cot_ref, vec_ref, *refs):
    pieces = refs[:n_down]
    out_ref, d_ref, sum_ref, keep_ref, send_ref, weights, turned, kept, result, sem, out_sem = refs[
        n_down:
    ]
    step = pl.program_id(0)
    tile, ff = hid_ref.shape[1:]

    @pl.when(step == 0)
    def _():
        for copy in piece_copies(where, pieces, weights, sem):
            copy.wait()
        sum_ref[...] = jnp.zeros_like(sum_ref)

    ffn = mm(hid_ref[0], weights[0], NT) + mm(hid_ref[1], weights[1], NT)
    resid = z_ref[...] * vec_ref[1:2] + vec_ref[2:3] + ffn + vec_ref[3:4]
    z, inverse = row_norm(resid)
    out_ref[...] = (z * vec_ref[4:5] + vec_ref[5:6]).astype(BF)
    cot = cot_ref[...].astype(F32)
    d_two = row_norm_back(cot, z, inverse, vec_ref[4:5])
    d_ref[...] = d_two
    sum_ref[0:1] += column_sum(cot * z)
    sum_ref[1:2] += column_sum(cot)
    sum_ref[2:3] += column_sum(d_two)
    rows = pl.ds(pl.multiple_of(step * tile, tile), tile)
    turned[:, rows] = d_two.astype(BF).T
    kept[:, rows, :] = hid_ref[...]

    @pl.when(step == pl.num_programs(0) - 1)
    def _():
        for half in range(2):
            for at in range(0, ff, 512):
                result[half, :, at : at + 512] = mm(
                    turned[...], kept[half, :, at : at + 512], NN
                ).astype(BF)
            for copy in part_copies(where, result, half, keep_ref, send_ref, out_sem, staged):
                copy.start()
        for half in range(2):
            for copy in part_copies(where, result, half, keep_ref, send_ref, out_sem, staged):
                copy.wait()


def second_part(where, staged, hidden, z_one, cot, vectors, pieces, tile=256):
    _, seq, ff = hidden.shape
    d_model = z_one.shape[1]
    return pl.pallas_call(
        functools.partial(second_kernel, staged, len(pieces)),
        out_shape=(
            jax.ShapeDtypeStruct((seq, d_model), BF),
            jax.ShapeDtypeStruct((seq, d_model), F32),
            jax.ShapeDtypeStruct((8, d_model), F32),
            *part_shapes(staged, 2, d_model, ff),
        ),
        grid_spec=pltpu.PrefetchScalarGridSpec(
            num_scalar_prefetch=1,
            grid=(seq // tile,),
            in_specs=[
                halves_tile(tile, ff),
                row_tile(tile, d_model),
                row_tile(tile, d_model),
                whole_spec(vectors),
            ]
            + [ANYWHERE] * len(pieces),
            out_specs=[
                row_tile(tile, d_model),
                row_tile(tile, d_model),
                pl.BlockSpec((8, d_model), lambda i, w: (0, 0)),
                ANYWHERE,
                ANYWHERE,
            ],
            scratch_shapes=[
                pltpu.VMEM((2, d_model, ff), BF),
                pltpu.VMEM((d_model, seq), BF),
                pltpu.VMEM((2, seq, ff), BF),
                pltpu.VMEM((2, d_model, ff), BF),
                pltpu.SemaphoreType.DMA((8, 4)),
                pltpu.SemaphoreType.DMA((2, 16)),
            ],
        ),
        cost_estimate=pl.CostEstimate(
            flops=2 * seq * d_model * 4 * ff,
            transcendentals=seq,
            bytes_accessed=seq * (d_model * 12 + ff * 4) + d_model * 8 * ff,
        ),
        name="second_part",
    )(where, hidden, z_one, cot, vectors, *pieces)


def third_kernel(n_up, where, d_ref, slope_ref, z_ref, inv_ref, vec_ref, *refs):
    up_pieces, down_pieces = refs[:n_up], refs[n_up : 2 * n_up]
    pre_ref, low_ref, one_ref, ctx_ref, sum_ref, bias_ref, up, down, sem, down_sem = refs[2 * n_up :]
    step = pl.program_id(0)
    ff = slope_ref.shape[2]
    width = ctx_ref.shape[2]

    @pl.when(step == 0)
    def _():
        waits = piece_copies(where, down_pieces, down, down_sem)
        waits += piece_copies(where, up_pieces, up, sem)
        for copy in waits:
            copy.wait()
        sum_ref[...] = jnp.zeros_like(sum_ref)
        bias_ref[...] = jnp.zeros_like(bias_ref)

    d_two = d_ref[...]
    d_two_low = d_two.astype(BF)
    d_normed = d_two
    for half in range(2):
        for at in range(0, ff, 512):
            span = slice(at, at + 512)
            d_pre = mm(d_two_low, down[half, :, span], NN) * slope_ref[half, :, span].astype(F32)
            d_pre = d_pre.astype(BF)
            pre_ref[half, :, span] = d_pre
            bias_ref[half, 0:1, span] += column_sum(d_pre.astype(F32))
            d_normed = d_normed + mm(d_pre, up[half, :, width + at : width + at + 512], NT)
    z = z_ref[...]
    low_ref[...] = (z * vec_ref[1:2] + vec_ref[2:3]).astype(BF)
    d_one = row_norm_back(d_normed, z, inv_ref[:, 0:1], vec_ref[1:2])
    one_ref[...] = d_one
    sum_ref[0:1] += column_sum(d_normed * z)
    sum_ref[1:2] += column_sum(d_normed)
    sum_ref[2:3] += column_sum(d_one)
    d_one_low = d_one.astype(BF)
    for half in range(2):
        ctx_ref[half] = mm(d_one_low, up[half, :, :width], NN).astype(BF)


def third_part(where, d_two, slope, z_one, inv_one, vectors, up_pieces, down_pieces, width, tile=256):
    seq, d_model = d_two.shape
    ff = slope.shape[2]
    return pl.pallas_call(
        functools.partial(third_kernel, len(up_pieces)),
        out_shape=(
            jax.ShapeDtypeStruct((2, seq, ff), BF),
            jax.ShapeDtypeStruct((seq, d_model), BF),
            jax.ShapeDtypeStruct((seq, d_model), F32),
            jax.ShapeDtypeStruct((2, seq, width), BF),
            jax.ShapeDtypeStruct((8, d_model), F32),
            jax.ShapeDtypeStruct((2, 8, ff), F32),
        ),
        grid_spec=pltpu.PrefetchScalarGridSpec(
            num_scalar_prefetch=1,
            grid=(seq // tile,),
            in_specs=[
                row_tile(tile, d_model),
                halves_tile(tile, ff),
                row_tile(tile, d_model),
                row_tile(tile, 128),
                whole_spec(vectors),
            ]
            + [ANYWHERE] * (2 * len(up_pieces)),
            out_specs=[
                halves_tile(tile, ff),
                row_tile(tile, d_model),
                row_tile(tile, d_model),
                halves_tile(tile, width),
                pl.BlockSpec((8, d_model), lambda i, w: (0, 0)),
                pl.BlockSpec((2, 8, ff), lambda i, w: (0, 0, 0)),
            ],
            scratch_shapes=[
                pltpu.VMEM((2, d_model, width + ff), BF),
                pltpu.VMEM((2, d_model, ff), BF),
                pltpu.SemaphoreType.DMA((8, 4)),
                pltpu.SemaphoreType.DMA((8, 4)),
            ],
        ),
        cost_estimate=pl.CostEstimate(
            flops=2 * seq * d_model * 2 * (2 * ff + width),
            transcendentals=0,
            bytes_accessed=seq * (d_model * 14 + ff * 8) + d_model * 4 * (2 * ff + width),
        ),
        name="third_part",
    )(where, d_two, slope, z_one, inv_one, vectors, *up_pieces, *down_pieces)


def add(first, second):
    return (first.astype(F32) + second.astype(F32)).astype(BF)


def core_stage(keep, send):
    return move(send, MOVE_CORE), keep


def flip_stage(moves, got, keep):
    return move(add(keep[1], got[1]), moves), add(keep[0], got[0])


def z_stage(got, keep):
    parts = [move(add(keep[k], got[k]), moves) for k, moves in zip((1, 2, 3), MOVE_Z)]
    return parts, keep[0].astype(F32) + got[0].astype(F32)


def z_sum(parts, keep):
    return keep + parts[0].astype(F32) + parts[1].astype(F32) + parts[2].astype(F32)


def lane_mask(head, rows):
    lanes = lax.broadcasted_iota(jnp.int32, (rows, PAIR), 1)
    return (lanes < HD) if head == 0 else (lanes >= HD)


def attn_fwd_kernel(table, qkv_ref, ctx_ref, prob_ref):
    pair = pl.program_id(0)
    q_ref, k_ref, v_ref = (qkv_ref.at[:, n * PAIR : (n + 1) * PAIR] for n in range(3))
    lanes = lax.broadcasted_iota(jnp.int32, (1, HALF), 1)
    for half in range(2):
        rows = pl.ds(half * HALF, HALF)
        query = q_ref[rows, :] * jnp.asarray(HD**-0.5, BF)
        parts = []
        for head in range(2):
            at = (pair * 2 + head) * 4
            start = (half ^ table[at]) * HALF
            flags = [table[at + 1 + n] == 1 for n in range(3)]
            key_lo = k_ref[pl.ds(pl.multiple_of(start, BLOCK), BLOCK), :]
            key_hi = k_ref[pl.ds(pl.multiple_of(start + BLOCK, BLOCK), BLOCK), :]
            masked = jnp.where(lane_mask(head, HALF), query, jnp.zeros_like(query))
            score_lo = mm(key_lo, masked, NT)
            score_hi = mm(key_hi, masked[BLOCK:], NT)
            no_lo = jnp.where(
                lanes < BLOCK,
                jnp.where(flags[0], 0.0, -1e30),
                jnp.where(flags[1], 0.0, -1e30),
            ).astype(F32)
            no_hi = jnp.where(flags[2], 0.0, -1e30).astype(F32)
            top_lo = jnp.max(score_lo, axis=0, keepdims=True) + no_lo
            top_hi = jnp.max(score_hi, axis=0, keepdims=True) + no_hi
            top = jnp.concatenate(
                [top_lo[:, :BLOCK], jnp.maximum(top_lo[:, BLOCK:], top_hi)], axis=1
            )
            ref_lo = jnp.where(no_lo < 0.0, 1e30, top)
            ref_hi = jnp.where(no_hi < 0.0, 1e30, top[:, BLOCK:])
            exp_lo = jnp.exp(score_lo - ref_lo)
            exp_hi = jnp.exp(score_hi - ref_hi)
            sum_lo = jnp.sum(exp_lo, axis=0, keepdims=True)
            sum_hi = jnp.sum(exp_hi, axis=0, keepdims=True)
            total = jnp.concatenate([sum_lo[:, :BLOCK], sum_lo[:, BLOCK:] + sum_hi], axis=1)
            scale = jnp.where(total > 0.0, 1.0 / jnp.where(total > 0.0, total, 1.0), 0.0)
            prob_lo = (exp_lo * scale).astype(BF)
            prob_hi = (exp_hi * scale[:, BLOCK:]).astype(BF)
            prob_ref[0, head, half, :, :HALF] = prob_lo
            prob_ref[0, head, half, :, HALF:] = prob_hi
            val_lo = v_ref[pl.ds(pl.multiple_of(start, BLOCK), BLOCK), :].T
            val_hi = v_ref[pl.ds(pl.multiple_of(start + BLOCK, BLOCK), BLOCK), :].T
            side = slice(head * HD, (head + 1) * HD)
            out_lo = mm(val_lo[side], prob_lo, NN)
            out_hi = mm(val_hi[side], prob_hi, NN)
            parts.append(
                jnp.concatenate([out_lo[:, :BLOCK], out_lo[:, BLOCK:] + out_hi], axis=1)
            )
        ctx_ref[rows, :] = jnp.concatenate(parts, axis=0).T.astype(BF)


def attn_fwd(table, proj):
    seq, width = proj.shape
    pairs = width // 3 // PAIR
    return pl.pallas_call(
        attn_fwd_kernel,
        out_shape=(
            jax.ShapeDtypeStruct((seq, width // 3), BF),
            jax.ShapeDtypeStruct((pairs, 2, 2, BLOCK, HALF + BLOCK), BF),
        ),
        grid_spec=pltpu.PrefetchScalarGridSpec(
            num_scalar_prefetch=1,
            grid=(pairs,),
            in_specs=[pl.BlockSpec((seq, 3 * PAIR), lambda p, t: (0, p))],
            out_specs=[
                pl.BlockSpec((seq, PAIR), lambda p, t: (0, p)),
                pl.BlockSpec((1, 2, 2, BLOCK, HALF + BLOCK), lambda p, t: (p, 0, 0, 0, 0)),
            ],
        ),
        cost_estimate=pl.CostEstimate(
            flops=pairs * 4 * 2 * 2 * 3 * BLOCK * BLOCK * PAIR,
            transcendentals=pairs * 4 * 3 * BLOCK * BLOCK,
            bytes_accessed=pairs * 4 * 3 * BLOCK * BLOCK * 2 + seq * width * 3,
        ),
        name="attn_fwd",
    )(table, proj)


def attn_bwd_kernel(table, qkv_ref, d_ref, prob_ref, out_ref, sum_ref, k_acc, v_acc):
    pair = pl.program_id(0)
    q_ref, k_ref, v_ref = (qkv_ref.at[:, n * PAIR : (n + 1) * PAIR] for n in range(3))
    for half in range(2):
        rows = pl.ds(half * HALF, HALF)
        query = q_ref[rows, :] * jnp.asarray(HD**-0.5, BF)
        d_ctx = d_ref[rows, :]
        parts = []
        for head in range(2):
            at = (pair * 2 + head) * 4
            start = (half ^ table[at]) * HALF
            at_lo = pl.ds(pl.multiple_of(start, BLOCK), BLOCK)
            at_hi = pl.ds(pl.multiple_of(start + BLOCK, BLOCK), BLOCK)
            keep = lane_mask(head, HALF)
            query_h = jnp.where(keep, query, jnp.zeros_like(query))
            d_ctx_h = jnp.where(keep, d_ctx, jnp.zeros_like(d_ctx))
            prob_lo = prob_ref[0, head, half, :, :HALF]
            prob_hi = prob_ref[0, head, half, :, HALF:]
            d_w_lo = mm(v_ref[at_lo, :], d_ctx_h, NT)
            d_w_hi = mm(v_ref[at_hi, :], d_ctx_h[BLOCK:], NT)
            wide_lo = prob_lo.astype(F32)
            wide_hi = prob_hi.astype(F32)
            dot_lo = jnp.sum(wide_lo * d_w_lo, axis=0, keepdims=True)
            dot_hi = jnp.sum(wide_hi * d_w_hi, axis=0, keepdims=True)
            dot = jnp.concatenate([dot_lo[:, :BLOCK], dot_lo[:, BLOCK:] + dot_hi], axis=1)
            d_s_lo = (wide_lo * (d_w_lo - dot)).astype(BF)
            d_s_hi = (wide_hi * (d_w_hi - dot[:, BLOCK:])).astype(BF)
            dk_lo = mm(d_s_lo, query_h, NN)
            dk_hi = mm(d_s_hi, query_h[BLOCK:], NN)
            dv_lo = mm(prob_lo, d_ctx_h, NN)
            dv_hi = mm(prob_hi, d_ctx_h[BLOCK:], NN)
            k_acc[head, at_lo, :] = dk_lo
            k_acc[head, at_hi, :] = dk_hi
            v_acc[head, at_lo, :] = dv_lo
            v_acc[head, at_hi, :] = dv_hi
            key_lo = k_ref[at_lo, :].T
            key_hi = k_ref[at_hi, :].T
            side = slice(head * HD, (head + 1) * HD)
            dq_lo = mm(key_lo[side], d_s_lo, NN)
            dq_hi = mm(key_hi[side], d_s_hi, NN)
            parts.append(jnp.concatenate([dq_lo[:, :BLOCK], dq_lo[:, BLOCK:] + dq_hi], axis=1))
        out_ref[rows, :PAIR] = (jnp.concatenate(parts, axis=0).T * HD**-0.5).astype(BF)
    out_ref[:, PAIR : 2 * PAIR] = (k_acc[0] + k_acc[1]).astype(BF)
    out_ref[:, 2 * PAIR :] = (v_acc[0] + v_acc[1]).astype(BF)
    sums = jnp.sum(out_ref[...].astype(F32), axis=0, keepdims=True)
    sum_ref[0] = jnp.broadcast_to(sums, sum_ref.shape[1:])


def attn_bwd(table, proj, d_context, probs):
    seq, width = proj.shape
    pairs = width // 3 // PAIR
    return pl.pallas_call(
        attn_bwd_kernel,
        out_shape=(
            jax.ShapeDtypeStruct((seq, width), BF),
            jax.ShapeDtypeStruct((pairs, 8, 3 * PAIR), F32),
        ),
        grid_spec=pltpu.PrefetchScalarGridSpec(
            num_scalar_prefetch=1,
            grid=(pairs,),
            in_specs=[
                pl.BlockSpec((seq, 3 * PAIR), lambda p, t: (0, p)),
                pl.BlockSpec((seq, PAIR), lambda p, t: (0, p)),
                pl.BlockSpec((1, 2, 2, BLOCK, HALF + BLOCK), lambda p, t: (p, 0, 0, 0, 0)),
            ],
            out_specs=[
                pl.BlockSpec((seq, 3 * PAIR), lambda p, t: (0, p)),
                pl.BlockSpec((1, 8, 3 * PAIR), lambda p, t: (p, 0, 0)),
            ],
            scratch_shapes=[pltpu.VMEM((2, seq, PAIR), F32)] * 2,
        ),
        cost_estimate=pl.CostEstimate(
            flops=pairs * 4 * 4 * 2 * 3 * BLOCK * BLOCK * PAIR,
            transcendentals=0,
            bytes_accessed=pairs * 4 * 3 * BLOCK * BLOCK * 2 + seq * width * 5,
        ),
        name="attn_bwd",
    )(table, proj, d_context, probs)


def gelu_both(values):
    half = 0.5 * (1.0 + lax.erf(values * (0.5**0.5)))
    slope = half + values * jnp.exp(-0.5 * values * values) * 0.3989422804014327
    return values * half, slope


def body(
    dp_size,
    tokens,
    grad_out,
    head_perm,
    block_mask,
    w_qkv,
    b_qv,
    w_out,
    b_out,
    gain_one,
    shift_one,
    w_up,
    b_up,
    w_down,
    b_down,
    gain_two,
    shift_two,
):
    seq = tokens.shape[0] // head_perm.shape[0]
    rows = w_qkv.shape[0]
    width = w_qkv.shape[2]
    d_model = tokens.shape[1]
    dp_at = lax.axis_index("dp")
    mp_at = lax.axis_index("mp")
    where = jnp.stack([dp_at // 4, (dp_at // 2) % 2, dp_at % 2]).astype(jnp.int32)

    own_tokens = lax.dynamic_slice_in_dim(tokens, mp_at * seq, seq, 0)
    own_grad = lax.dynamic_slice_in_dim(grad_out, mp_at * seq, seq, 0)
    table = jnp.concatenate([head_perm[:, :, None], block_mask], axis=2).astype(jnp.int32)
    table = table.reshape(2, -1)
    table_own = lax.dynamic_index_in_dim(table, mp_at, 0, keepdims=False)
    table_other = swap_mp(lax.dynamic_index_in_dim(table, 1 - mp_at, 0, keepdims=False))

    small = jnp.stack(
        [
            b_out,
            gain_one,
            shift_one,
            b_down,
            gain_two,
            shift_two,
            b_up[:rows],
            b_up[rows:],
            b_qv.reshape(-1),
        ],
        axis=1,
    )
    small = jnp.pad(small, ((0, 0), (0, SMALL - small.shape[1])))
    pairs = width // PAIR
    by_pair = w_qkv.reshape(rows, 3, pairs, PAIR).transpose(0, 2, 1, 3).reshape(rows, 3 * width)
    shard_qkv = jnp.concatenate([by_pair, small], axis=1)
    shard_up = jnp.concatenate([w_out.T, w_up], axis=1)
    shard_down = w_down.T
    staged = dp_size == 16

    def plain_gather(shard):
        full = lax.all_gather(shard, "dp", axis=0, tiled=True)
        return full, swap_mp(full)

    def gather_z(shard):
        return jnp.stack([shard] + [move(shard, moves) for moves in MOVE_Z])

    def gather_core(*pieces):
        return (*pieces, *(move(piece, MOVE_CORE) for piece in pieces))

    if staged:
        qkv_z = gather_z(shard_qkv)
        qkv_a = move(qkv_z, MOVE_FIRST)
        up_z = gather_z(after(shard_up, qkv_z))
        qkv_b, qkv_c = move(qkv_z, MOVE_SECOND), move(qkv_a, MOVE_SECOND)
        up_z, down_in = lax.optimization_barrier((up_z, shard_down))
        down_z = gather_z(down_in)
        up_a = move(after(up_z, qkv_b, qkv_c), MOVE_FIRST)
        qkv_own, qkv_other = assemble(where, gather_core(qkv_z, qkv_a, qkv_b, qkv_c))
    else:
        qkv_own, qkv_other = plain_gather(shard_qkv)

    small_own = qkv_own[:, 3 * width :].astype(F32)
    small_other = qkv_other[:, 3 * width :].astype(F32)
    vectors = small_own.T[:8]

    def up_bias(columns):
        return columns[:, 6:8].reshape(dp_size, rows, 2).transpose(0, 2, 1).reshape(1, -1)

    def qkv_bias(columns):
        parts = columns[:, 8].reshape(dp_size, 2, rows // 2).transpose(1, 0, 2)
        parts = parts.reshape(2, pairs, PAIR)
        return jnp.stack([parts[0], jnp.zeros_like(parts[0]), parts[1]], axis=1).reshape(1, -1)

    wq = (qkv_own[:, : 3 * width], qkv_other[:, : 3 * width])
    bias_up = jnp.stack([up_bias(small_own), up_bias(small_other)])

    def project(w, s):
        return (mm(own_tokens, w, NN) + qkv_bias(s)).astype(BF)

    proj_own = project(wq[0], small_own)
    if staged:
        table_own, up_a = lax.optimization_barrier((table_own, up_a))
        up_b, up_c = move(up_z, MOVE_SECOND), move(up_a, MOVE_SECOND)
    ctx_own, probs_own = attn_fwd(table_own, proj_own)
    proj_other = project(after(wq[1], ctx_own), small_other)
    if staged:
        table_other, up_b, up_c, down_z, proj_other = lax.optimization_barrier(
            (table_other, up_b, up_c, down_z, proj_other)
        )
        down_a = move(down_z, MOVE_FIRST)
        up_pieces = gather_core(up_z, up_a, up_b, up_c)
    else:
        up_pieces = plain_gather(shard_up)
    ctx_other, probs_other = attn_fwd(table_other, proj_other)
    tables, proj = (table_own, table_other), (proj_own, proj_other)
    probs = (probs_own, probs_other)
    if staged:
        down_a, ctx_other = lax.optimization_barrier((down_a, ctx_other))
        down_b, down_c = move(down_z, MOVE_SECOND), move(down_a, MOVE_SECOND)
    ctx = (ctx_own, ctx_other)
    z_one, inv_one, hidden, slope = first_part(where, own_tokens, ctx, vectors, bias_up, up_pieces)
    if staged:
        hidden, down_b, down_c = lax.optimization_barrier((hidden, down_b, down_c))
        down_pieces = gather_core(down_z, down_a, down_b, down_c)
    else:
        down_pieces = plain_gather(shard_down)

    out_own, d_two, sums_two, *down_parts = second_part(
        where, staged, hidden, z_one, own_grad, vectors, down_pieces
    )
    out_other = swap_mp(out_own)

    def plain_scatter(whole):
        own, other = (whole[0], whole[1]) if isinstance(whole, tuple) else whole
        summed = own.astype(F32) + swap_mp(other).astype(F32)
        return lax.psum_scatter(summed, "dp", scatter_dimension=0, tiled=True)

    if staged:
        down_got, down_keep = core_stage(*down_parts)
        d_two, down_got = lax.optimization_barrier((d_two, down_got))
        down_got, down_keep = flip_stage(MOVE_REDUCE[0], down_got, down_keep)
    else:
        s_down = plain_scatter(down_parts[0])
    d_pre, normed_low, d_one, d_ctx, sums_one, sums_up = third_part(
        where, d_two, slope, z_one, inv_one, vectors, up_pieces, down_pieces, width
    )
    d_one_low = d_one.astype(BF)
    shared = jnp.concatenate(
        [sums_one[2:3], sums_one[0:2], sums_two[2:3], sums_two[0:2]], axis=0
    )

    def columns(stacked):
        return jnp.pad(stacked, ((0, SMALL - stacked.shape[0]), (0, 0))).T.astype(BF)

    def vector_grads(g_up_bias):
        per_up = g_up_bias.reshape(dp_size, 2, rows).transpose(1, 0, 2).reshape(2, d_model)
        return columns(jnp.concatenate([shared, per_up], axis=0))

    def qv_grads(sums):
        sums = sums[:, 0].reshape(pairs, 3, PAIR).transpose(1, 0, 2).reshape(3, width)
        qv = jnp.stack([sums[0], sums[2]]).reshape(2, dp_size, rows // 2)
        return columns(qv.transpose(1, 0, 2).reshape(1, d_model))

    small_up = jnp.stack([vector_grads(sums_up[n, 0]) for n in range(2)])
    up_parts = grads(
        where, staged, [normed_low, d_one_low], [(d_pre, d_pre), ctx], small_up
    )
    if staged:
        up_got, up_keep = core_stage(*up_parts)
        table_other, down_got, up_keep = lax.optimization_barrier((tables[1], down_got, up_keep))
        down_got, down_keep = flip_stage(MOVE_REDUCE[1], down_got, down_keep)
        tables = (tables[0], table_other)
    else:
        s_up = plain_scatter(up_parts[0])
    d_proj_other, sums_other = attn_bwd(tables[1], proj[1], d_ctx[1], probs[1])
    small_qkv_other = qv_grads(sums_other)
    other_parts = grads(where, staged, [own_tokens], [(d_proj_other,)], small_qkv_other[None])
    if staged:
        qo_got, qo_keep = core_stage(*other_parts)
        table_own, up_got, down_got, qo_keep = lax.optimization_barrier(
            (tables[0], up_got, down_got, qo_keep)
        )
        down_parts, down_keep = z_stage(down_got, down_keep)
        up_got, up_keep = flip_stage(MOVE_REDUCE[0], up_got, up_keep)
        tables = (table_own, tables[1])
    d_proj_own, sums_own = attn_bwd(tables[0], proj[0], d_ctx[0], probs[0])
    small_qkv_own = qv_grads(sums_own)
    if staged:
        d_proj_own, qo_got, up_got = lax.optimization_barrier((d_proj_own, qo_got, up_got))
        up_got, up_keep = flip_stage(MOVE_REDUCE[1], up_got, up_keep)
        qo_got, qo_keep = flip_stage(MOVE_Y, qo_got, qo_keep)
    d_input = mm(d_proj_own, wq[0], NT) + mm(d_proj_other, wq[1], NT) + d_one
    in_low = d_input.astype(BF)
    tokens_in = own_tokens
    if staged:
        in_low, tokens_in = lax.optimization_barrier((in_low, own_tokens))
    in_other = swap_mp(in_low).astype(F32)
    own_parts = grads(where, staged, [tokens_in], [(d_proj_own,)], small_qkv_own[None])
    if staged:
        qs_got, qs_keep = core_stage(*own_parts)
        s_down = z_sum(down_parts, down_keep)
        up_parts, up_keep = z_stage(up_got, up_keep)
        qs_got, qs_keep = flip_stage(MOVE_Y, qs_got, qs_keep)
        qo_parts, qo_keep = z_stage(qo_got, qo_keep)
        s_up = z_sum(up_parts, up_keep)
        qo_sum = move(z_sum(qo_parts, qo_keep).astype(BF), MOVE_X)
        qs_parts, qs_keep = z_stage(qs_got, qs_keep)
        s_qkv = (z_sum(qs_parts, qs_keep) + qo_sum.astype(F32))[0]
    else:
        s_qkv = plain_scatter((own_parts[0][0], other_parts[0][0]))

    def place(own, other):
        whole = jnp.zeros((2 * seq, d_model), own.dtype)
        whole = lax.dynamic_update_slice_in_dim(whole, own, mp_at * seq, 0)
        return lax.dynamic_update_slice_in_dim(whole, other, (1 - mp_at) * seq, 0)

    ff = w_up.shape[1]
    cols = s_up[:, ff + width :].T
    g_w_qkv = s_qkv[:, : 3 * width].reshape(rows, pairs, 3, PAIR).transpose(0, 2, 1, 3)
    return (
        place(out_own, out_other),
        place(d_input, in_other),
        g_w_qkv.reshape(rows, 3, width),
        s_qkv[:, 3 * width].reshape(2, rows // 2),
        s_up[:, ff : ff + width].T,
        cols[0],
        cols[1],
        cols[2],
        s_up[:, :ff],
        cols[6:8].reshape(-1),
        s_down.T,
        cols[3],
        cols[4],
        cols[5],
    )


def solution(mesh):
    placed = (
        P("dp", None),
        P("dp", None),
        P("dp", "mp"),
        P("dp", "mp", None),
        P("dp", None, "mp"),
        P(None, ("mp", "dp")),
        P("mp", "dp"),
        P("dp"),
        P("dp"),
        P("dp"),
        P("dp", "mp"),
        P(("mp", "dp")),
        P("mp", "dp"),
        P("dp"),
        P("dp"),
        P("dp"),
    )
    return jax.shard_map(
        functools.partial(body, mesh.shape["dp"]),
        mesh=mesh,
        in_specs=placed,
        out_specs=(
            P("dp", None),
            P("dp", None),
            P("dp", None, "mp"),
            P(None, ("mp", "dp")),
            P("mp", "dp"),
            P("dp"),
            P("dp"),
            P("dp"),
            P("dp", "mp"),
            P(("mp", "dp")),
            P("mp", "dp"),
            P("dp"),
            P("dp"),
            P("dp"),
        ),
        check_vma=False,
    )
```

time: 486 us -> 392 us (0.81)
  matrix products: 97.1 us -> 18.2 us
  waiting for transfers between devices: 145 us -> 68 us
  Pallas kernels: 73.6 us -> 143 us
  starting transfers between devices: 60 us -> 70 us
  local copies, waits for them, and re-layouts: 51.5 us -> 43.3 us
    dot_general x24 -> x4, matrix products: 97.1 us -> 18.2 us  [mm(): return lax.dot_general(first, second, dims, preferred_element_type=F32)]
    pallas_call x8 -> x9, Pallas kernels: 55.6 us -> 125 us  [the longest x3 30.8 us: grads(): pl.pallas_call(functools.partial(grads_kernel, staged, halves, widths), o...]
    ppermute x3, waiting for transfers between devices: 52.3 us -> 0.01 us  [swap_mp(): return lax.ppermute(values, 'mp', [(0, 1), (1, 0)])]
    ppermute x48 -> x53, waiting for transfers between devices: 93 us -> 68 us  [move(): return lax.ppermute(values, AXES, moves)]
    unnamed x81 -> x56, local copies, waits for them, and re-layouts: 21.1 us -> 7.38 us
    reduce_sum x8 -> x0, other arithmetic: 10.7 us -> none  [the longest x2 4.71 us: small_grads(): sums = jnp.sum(d, axis=0, dtype=F32)]
    concatenate x5 -> x1, other arithmetic: 10.1 us -> 0.93 us  [body(): shard_up = jnp.concatenate([w_out.T, w_up], axis=1)]
    ppermute x48 -> x53, starting transfers between devices: 56.7 us -> 64.5 us  [move(): return lax.ppermute(values, AXES, moves)]
  transfers between devices with their start and end apart: 51 -> 56, of which waited for: 15 -> 16; matrix products, arithmetic and copies ran while one was open for 18% -> 22% of each run, Pallas kernels for 8% -> 31%
where the time goes in v2:
time: 392 us; the launch traced here: 388 us
  Pallas kernels  143 us (36%)
  starting transfers between devices  70 us (18%)
  waiting for transfers between devices  68 us (17%)
  other arithmetic  43.7 us (11%)
  local copies, waits for them, and re-layouts  43.3 us (11%)
  matrix products  18.2 us (5%)
    ppermute x53, waiting for transfers between devices, move(): return lax.ppermute(values, AXES, moves)  68 us
    ppermute x53, starting transfers between devices, move(): return lax.ppermute(values, AXES, moves)  64.5 us
    pallas_call x3, Pallas kernels, grads(): pl.pallas_call(functools.partial(grads_kernel, staged, halves, widths), o...  30.8 us
    pallas_call x1, Pallas kernels, third_part(): pl.pallas_call(functools.partial(third_kernel, len(up_pieces)), out_shape...  25.6 us
    convert_element_type x11, other arithmetic, add(): return (first.astype(F32) + second.astype(F32)).astype(BF)  22.5 us
    pallas_call x2, Pallas kernels, attn_bwd(): pl.pallas_call(attn_bwd_kernel, out_shape=(jax.ShapeDtypeStruct((seq, wid...  22.3 us
    pallas_call x1, Pallas kernels, second_part(): pl.pallas_call(functools.partial(second_kernel, staged, len(pieces)), out...  21.4 us
    pallas_call x1, Pallas kernels, first_part(): pl.pallas_call(functools.partial(first_kernel, len(pieces)), out_shape=(j...  19.6 us
  transfers between devices with their start and end apart: 56, of which 16 were waited for; matrix products, arithmetic and copies ran while one was open for 22% of the time, Pallas kernels for 31%

profile of v2, /device:TPU:0, one launch (start us, length us, event | category | flops | bytes accessed | tf_op | source)
XLA Modules:
  0.0 387.5 jit_solution(10936980775737098030)
XLA Ops:
  13.9 4.4 %collective-permute-done.1 = bf16[48,1280]{1,0:T(8,128)(2,1)S(1)} collective-permute-done((bf16[48,1280]{1,0:T(8,128)(2,1)S(1)}, bf16[48,1280]{1,0:T(8,128)(2,1)S(1)}, u32[]{:S(2)}, u32[]{:S(2)}) %collective-permute-start.1) | collective-permute-done | bytes 122912 | tf_op jit(solution)/shard_map/ppermute | solution.py:49
  31.4 6.2 %collective-permute-done.4 = bf16[48,1920]{1,0:T(8,128)(2,1)S(1)} collective-permute-done((bf16[48,1920]{1,0:T(8,128)(2,1)S(1)}, bf16[48,1920]{1,0:T(8,128)(2,1)S(1)}, u32[]{:S(2)}, u32[]{:S(2)}) %collective-permute-start.4) | collective-permute-done | bytes 184352 | tf_op jit(solution)/shard_map/ppermute | solution.py:49
  38.6 4.4 %collective-permute-start.17 = (bf16[48,1536]{1,0:T(8,128)(2,1)}, bf16[48,1536]{1,0:T(8,128)(2,1)S(1)}, u32[]{:S(2)}, u32[]{:S(2)}) collective-permute-start(bf16[48,1536]{1,0:T(8,128)(2,1)} %bitcast.285), channel_id=1, source_target_pairs={{0,8},{1,9},{2,10},{3,11},{4,12},{5,13},{6,14},{7,15},{8,16},{9,17... | collective-permute-start | bytes 442376 | tf_op jit(solution)/shard_map/ppermute | solution.py:49
  65.2 5.2 %assemble.1 = (bf16[768,1280]{1,0:T(8,128)(2,1)}, bf16[768,1280]{1,0:T(8,128)(2,1)}) custom-call(s32[3]{0:T(128)} %pad_add_fusion.1.where, bf16[4,48,1280]{2,1,0:T(8,128)(2,1)} %pad_maximum_fusion.2.refs_0_, bf16[4,48,1280]{2,1,0:T(8,128)(2,1)} %collective-permute-done.7.refs_1_, bf16[4,48,1280]{2,1,0:T(8,128)(2,1)} %collective-permute-done.6.refs_2_, ...), custom_call_target="tpu_custom_call" | custom-call | bytes 7864320 | tf_op jit(solution)/shard_map/assemble/pallas_call | solution.py:114
  70.4 4.2 %copy.94 = bf16[768,1280]{0,1:T(8,128)(2,1)} copy(bf16[768,1280]{1,0:T(8,128)(2,1)} %get-tuple-element.80) | data formatting | bytes 3932160 | tf_op jit(solution)/shard_map/assemble/pallas_call | solution.py:114
  77.7 4.5 %collective-permute-done.9.refs_1_ = bf16[4,48,1920]{2,1,0:T(8,128)(2,1)} collective-permute-done((bf16[4,48,1920]{2,1,0:T(8,128)(2,1)}, bf16[4,48,1920]{2,1,0:T(8,128)(2,1)}, u32[]{:S(2)}, u32[]{:S(2)}) %collective-permute-start.9) | collective-permute-done | bytes 737312 | tf_op jit(solution)/shard_map/ppermute | solution.py:49
  82.1 5.2 %add_convert_fusion.1.qkv_ref = bf16[1024,1152]{1,0:T(8,128)(2,1)} fusion(bf16[1024,768]{1,0:T(8,128)(2,1)} %constant_dynamic-slice_fusion.3.tok_ref.refs_0_, f32[1152]{0:T(1024)S(1)} %add.322, bf16[768,1280]{1,0:T(8,128)(2,1)S(1)} %copy-done.3), kind=kOutput, calls=%fused_computation.1 | convolution fusion | flops 1814298624 | bytes 5709824 | tf_op jit(solution)/shard_map/dot_general | solution.py:25
  88.7 8.9 %attn_fwd.2 = (bf16[1024,384]{1,0:T(8,128)(2,1)}, bf16[3,2,2,256,768]{4,3,2,1,0:T(8,128)(2,1)}) custom-call(s32[24]{0:T(128)} %get-tuple-element.122.table, bf16[1024,1152]{1,0:T(8,128)(2,1)} %add_convert_fusion.1.qkv_ref), custom_call_target="tpu_custom_call" | custom-call | flops 1207959552 | bytes 8257536 | tf_op jit(solution)/shard_map/attn_fwd/pallas_call | solution.py:585
  97.6 5.6 %add_convert_fusion.qkv_ref = bf16[1024,1152]{1,0:T(8,128)(2,1)} fusion(bf16[1024,768]{1,0:T(8,128)(2,1)} %constant_dynamic-slice_fusion.3.tok_ref.refs_0_, bf16[768,1152]{1,0:T(8,128)(2,1)} %slice.332, f32[1152]{0:T(1024)S(1)} %add.326), kind=kOutput, calls=%fused_computation | convolution fusion | flops 1814298624 | bytes 5706240 | tf_op jit(solution)/shard_map/dot_general | solution.py:25
  106.5 8.9 %attn_fwd.3 = (bf16[1024,384]{1,0:T(8,128)(2,1)}, bf16[3,2,2,256,768]{4,3,2,1,0:T(8,128)(2,1)}) custom-call(s32[24]{0:T(128)} %copy-done.26, bf16[1024,1152]{1,0:T(8,128)(2,1)} %add_convert_fusion.qkv_ref), custom_call_target="tpu_custom_call" | custom-call | flops 1207959552 | bytes 8257536 | tf_op jit(solution)/shard_map/attn_fwd/pallas_call | solution.py:585
  119.2 19.6 %first_part.1 = (f32[1024,768]{1,0:T(8,128)}, f32[1024,128]{1,0:T(8,128)}, bf16[2,1024,1536]{2,1,0:T(8,128)(2,1)}, bf16[2,1024,1536]{2,1,0:T(8,128)(2,1)}) custom-call(s32[3]{0:T(128)} %pad_add_fusion.1.where, bf16[1024,768]{1,0:T(8,128)(2,1)} %constant_dynamic-slice_fusion.3.tok_ref.refs_0_, bf16[1024,384]{1,0:T(8,128)(2,1)} %get-tuple-element.81.ctx0_ref.refs_4_, ...), custom_call_target="tpu_custom_call" | custom-call | flops 6039797760 | bytes 24772608 | tf_op jit(solution)/shard_map/first_part/pallas_call | solution.py:291
  143.8 21.4 %second_part.1 = (bf16[1024,768]{1,0:T(8,128)(2,1)}, f32[1024,768]{1,0:T(8,128)}, f32[8,768]{1,0:T(8,128)}, bf16[2,2,4,48,1536]{4,3,2,1,0:T(8,128)(2,1)}, bf16[2,2,4,48,1536]{4,3,2,1,0:T(8,128)(2,1)}) custom-call(s32[3]{0:T(128)} %pad_add_fusion.1.where, bf16[2,1024,1536]{2,1,0:T(8,128)(2,1)} %get-tuple-element.95.hid_ref, ...), custom_call_target="tpu_custom_call" | custom-call | flops 9663676416 | bytes 25165824 | tf_op jit(solution)/shard_map/second_part/pallas_call | solution.py:375
  170.1 25.6 %third_part.1 = (bf16[2,1024,1536]{2,1,0:T(8,128)(2,1)}, bf16[1024,768]{1,0:T(8,128)(2,1)}, f32[1024,768]{1,0:T(8,128)}, bf16[2,1024,384]{2,1,0:T(8,128)(2,1)}, f32[8,768]{1,0:T(8,128)}, /*index=5*/f32[2,8,1536]{2,1,0:T(8,128)}) custom-call(s32[3]{0:T(128)} %pad_add_fusion.1.where, f32[1024,768]{1,0:T(8,128)} %get-tuple-element.102.d_ref, ...), custom_call_target="tpu_custom_call" | custom-call | flops 10871635968 | bytes 34209792 | tf_op jit(solution)/shard_map/third_part/pallas_call | solution.py:460
  203.1 16.9 %grads.3 = (bf16[2,2,4,48,2048]{4,3,2,1,0:T(8,128)(2,1)}, bf16[2,2,4,48,2048]{4,3,2,1,0:T(8,128)(2,1)}) custom-call(s32[3]{0:T(128)} %pad_add_fusion.1.where, bf16[1024,768]{1,0:T(8,128)(2,1)} %get-tuple-element.105.refs_0_, bf16[1024,768]{1,0:T(8,128)(2,1)} %convert_element_type.779.refs_1_, bf16[2,1024,1536]{2,1,0:T(8,128)(2,1)} %get-tuple-element.107.refs_2_.refs_3_, ...), custom_call_target="tpu_custom_call" | custom-call | flops 6039797760 | bytes 14680064 | tf_op jit(solution)/shard_map/grads/pallas_call | solution.py:208
  220.2 4.1 %add_convert_fusion.5 = (bf16[1,2,4,48,1536]{4,3,2,1,0:T(8,128)(2,1)S(1)}, bf16[2,4,48,1536]{3,2,1,0:T(8,128)(2,1)}) fusion(bf16[2,2,4,48,1536]{4,3,2,1,0:T(8,128)(2,1)} %collective-permute-done.32, bf16[2,2,4,48,1536]{4,3,2,1,0:T(8,128)(2,1)} %get-tuple-element.112), kind=kLoop, calls=%fused_computation.7 | loop fusion | flops 4718592 | bytes 7077888 | tf_op jit(solution)/shard_map/convert_element_type | solution.py:506
  231.1 9.7 %collective-permute-done.34 = bf16[2,4,48,1536]{3,2,1,0:T(8,128)(2,1)} collective-permute-done((bf16[2,4,48,1536]{3,2,1,0:T(8,128)(2,1)}, bf16[2,4,48,1536]{3,2,1,0:T(8,128)(2,1)}, u32[]{:S(2)}, u32[]{:S(2)}) %collective-permute-start.34) | collective-permute-done | bytes 1179680 | tf_op jit(solution)/shard_map/ppermute | solution.py:49
  244.9 11.2 %attn_bwd.2 = (bf16[1024,1152]{1,0:T(8,128)(2,1)}, f32[3,8,384]{2,1,0:T(8,128)}) custom-call(s32[24]{0:T(128)} %copy-done.26, bf16[1024,1152]{1,0:T(8,128)(2,1)} %add_convert_fusion.qkv_ref, bf16[1024,384]{1,0:T(8,128)(2,1)} %get-tuple-element.172.d_ref, bf16[3,2,2,256,768]{4,3,2,1,0:T(8,128)(2,1)} %get-tuple-element.118.prob_ref), custom_call_target="tpu_custom_call" | custom-call | flops 2415919104 | bytes 10616832 | tf_op jit(solution)/shard_map/attn_bwd/pallas_call | solution.py:660
  258.1 6.8 %grads.4 = (bf16[2,4,1,48,1280]{4,3,2,1,0:T(8,128)(2,1)}, bf16[2,4,1,48,1280]{4,3,2,1,0:T(8,128)(2,1)}) custom-call(s32[3]{0:T(128)} %pad_add_fusion.1.where, bf16[1024,768]{1,0:T(8,128)(2,1)} %constant_dynamic-slice_fusion.3.tok_ref.refs_0_, bf16[1024,1152]{1,0:T(8,128)(2,1)} %get-tuple-element.119.refs_1_, bf16[1,768,128]{2,1,0:T(8,128)(2,1)} %pad_bitcast_fusion.1.refs_2_), custom_call_target="tpu_custom_call" | custom-call | flops 1811939328 | bytes 4587520 | tf_op jit(solution)/shard_map/grads/pallas_call | solution.py:208
  265.1 6.3 %add_convert_fusion.2 = (bf16[1,2,4,48,2048]{4,3,2,1,0:T(8,128)(2,1)}, bf16[2,4,48,2048]{3,2,1,0:T(8,128)(2,1)}) fusion(bf16[2,2,4,48,2048]{4,3,2,1,0:T(8,128)(2,1)} %collective-permute-done.33, bf16[2,2,4,48,2048]{4,3,2,1,0:T(8,128)(2,1)} %get-tuple-element.126), kind=kLoop, calls=%fused_computation.2 | loop fusion | flops 6291456 | bytes 9437184 | tf_op jit(solution)/shard_map/convert_element_type | solution.py:506
  281.7 11.1 %attn_bwd.3 = (bf16[1024,1152]{1,0:T(8,128)(2,1)}, f32[3,8,384]{2,1,0:T(8,128)}) custom-call(s32[24]{0:T(128)} %get-tuple-element.122.table, bf16[1024,1152]{1,0:T(8,128)(2,1)} %add_convert_fusion.1.qkv_ref, bf16[1024,384]{1,0:T(8,128)(2,1)} %get-tuple-element.171.d_ref, bf16[3,2,2,256,768]{4,3,2,1,0:T(8,128)(2,1)} %get-tuple-element.123.prob_ref), custom_call_target="tpu_custom_call" | custom-call | flops 2415919104 | bytes 10616832 | tf_op jit(solution)/shard_map/attn_bwd/pallas_call | solution.py:660
  310.3 7.0 %grads.5 = (bf16[2,4,1,48,1280]{4,3,2,1,0:T(8,128)(2,1)}, bf16[2,4,1,48,1280]{4,3,2,1,0:T(8,128)(2,1)}) custom-call(s32[3]{0:T(128)} %pad_add_fusion.1.where, bf16[1024,768]{1,0:T(8,128)(2,1)} %constant_dynamic-slice_fusion.3.tok_ref.refs_0_, bf16[1024,1152]{1,0:T(8,128)(2,1)} %get-tuple-element.128.refs_1_, bf16[1,768,128]{2,1,0:T(8,128)(2,1)} %pad_bitcast_fusion.refs_2_), custom_call_target="tpu_custom_call" | custom-call | flops 1811939328 | bytes 4587520 | tf_op jit(solution)/shard_map/grads/pallas_call | solution.py:208
  345.6 6.9 %collective-permute-done.51 = bf16[48,2048]{1,0:T(8,128)(2,1)S(1)} collective-permute-done((bf16[48,2048]{1,0:T(8,128)(2,1)S(1)}, bf16[48,2048]{1,0:T(8,128)(2,1)S(1)}, u32[]{:S(2)}, u32[]{:S(2)}) %collective-permute-start.51) | collective-permute-done | bytes 196640 | tf_op jit(solution)/shard_map/ppermute | solution.py:49
  358.2 9.2 %collective-permute-done.40 = bf16[4,1,48,1280]{3,2,0,1:T(8,128)(2,1)S(1)} collective-permute-done((bf16[4,1,48,1280]{3,2,0,1:T(8,128)(2,1)S(1)}, bf16[4,1,48,1280]{3,2,0,1:T(8,128)(2,1)S(1)}, u32[]{:S(2)}, u32[]{:S(2)}) %collective-permute-start.40) | collective-permute-done | bytes 491552 | tf_op jit(solution)/shard_map/ppermute | solution.py:49
  367.4 4.9 %collective-permute-start.41 = (bf16[1,48,1280]{2,1,0:T(8,128)(2,1)S(1)}, bf16[1,48,1280]{2,1,0:T(8,128)(2,1)S(1)}, u32[]{:S(2)}, u32[]{:S(2)}) collective-permute-start(bf16[1,48,1280]{2,1,0:T(8,128)(2,1)S(1)} %get-tuple-element.176), channel_id=1, source_target_pairs={{0,8},{1,9},{2,10},{3,11},{4,12},{5,13},{6,14},{7,15},{8,16},{9,17... | collective-permute-start | bytes 368648 | tf_op jit(solution)/shard_map/ppermute | solution.py:49
  (279 shorter events, 167.5 us)
Async XLA Ops:
  27.2 22.4 %collective-permute-start.6 = (bf16[4,48,1280]{2,1,0:T(8,128)(2,1)}, bf16[4,48,1280]{2,1,0:T(8,128)(2,1)}, u32[]{:S(2)}, u32[]{:S(2)}) collective-permute-start(bf16[4,48,1280]{2,1,0:T(8,128)(2,1)} %pad_maximum_fusion.2.refs_0_), channel_id=1, source_target_pairs={{0,4},{1,5},{2,3},{3,2},{4,0},{5,1},{6,7},{7,6},{8,12},{9,13},{10,... | collective-permute-start | bytes 1474568 | tf_op jit(solution)/shard_map/ppermute | solution.py:49
  28.7 21.4 %collective-permute-start.8 = (bf16[4,48,1280]{2,1,0:T(8,128)(2,1)}, bf16[4,48,1280]{2,1,0:T(8,128)(2,1)}, u32[]{:S(2)}, u32[]{:S(2)}) collective-permute-start(bf16[4,48,1280]{2,1,0:T(8,128)(2,1)} %collective-permute-done.7.refs_1_), channel_id=1, source_target_pairs={{0,4},{1,5},{2,3},{3,2},{4,0},{5,1},{6,7},{7,6},{8,12},{9,13},{10,... | collective-permute-start | bytes 1474568 | tf_op jit(solution)/shard_map/ppermute | solution.py:49
  45.8 18.7 %collective-permute-start.10 = (bf16[4,48,1280]{2,1,0:T(8,128)(2,1)}, bf16[4,48,1280]{2,1,0:T(8,128)(2,1)}, u32[]{:S(2)}, u32[]{:S(2)}) collective-permute-start(bf16[4,48,1280]{2,1,0:T(8,128)(2,1)} %pad_maximum_fusion.2.refs_0_), channel_id=1, source_target_pairs={{0,2},{1,3},{2,0},{3,1},{4,6},{5,7},{6,4},{7,5},{8,10},{9,11},{10,... | collective-permute-start | bytes 1474568 | tf_op jit(solution)/shard_map/ppermute | solution.py:49
  60.4 42.9 %collective-permute-start.14 = (s32[24]{0:T(128)S(1)}, s32[24]{0:T(128)S(1)}, u32[]{:S(2)}, u32[]{:S(2)}) collective-permute-start(s32[24]{0:T(128)S(1)} %get-tuple-element.185), channel_id=1, source_target_pairs={{0,1},{1,0},{2,3},{3,2},{4,5},{5,4},{6,7},{7,6},{8,9},{9,8},{10,11... | collective-permute-start | bytes 296 | tf_op jit(solution)/shard_map/ppermute | solution.py:53
  64.5 38.7 %collective-permute-start.15 = (bf16[4,48,1920]{2,1,0:T(8,128)(2,1)}, bf16[4,48,1920]{2,1,0:T(8,128)(2,1)}, u32[]{:S(2)}, u32[]{:S(2)}) collective-permute-start(bf16[4,48,1920]{2,1,0:T(8,128)(2,1)} %pad_maximum_fusion.refs_0_), channel_id=1, source_target_pairs={{0,4},{1,5},{2,3},{3,2},{4,0},{5,1},{6,7},{7,6},{8,12},{9,13},{10,... | collective-permute-start | bytes 2211848 | tf_op jit(solution)/shard_map/ppermute | solution.py:49
  64.5 52.5 %collective-permute-start.21 = (bf16[4,48,1920]{2,1,0:T(8,128)(2,1)}, bf16[4,48,1920]{2,1,0:T(8,128)(2,1)}, u32[]{:S(2)}, u32[]{:S(2)}) collective-permute-start(bf16[4,48,1920]{2,1,0:T(8,128)(2,1)} %pad_maximum_fusion.refs_0_), channel_id=1, source_target_pairs={{0,2},{1,3},{2,0},{3,1},{4,6},{5,7},{6,4},{7,5},{8,10},{9,11},{10,... | collective-permute-start | bytes 2211848 | tf_op jit(solution)/shard_map/ppermute | solution.py:49
  64.6 17.5 %collective-permute-start.9 = (bf16[4,48,1920]{2,1,0:T(8,128)(2,1)}, bf16[4,48,1920]{2,1,0:T(8,128)(2,1)}, u32[]{:S(2)}, u32[]{:S(2)}) collective-permute-start(bf16[4,48,1920]{2,1,0:T(8,128)(2,1)} %pad_maximum_fusion.refs_0_), channel_id=1, source_target_pairs={{0,1},{1,0},{2,6},{3,7},{4,5},{5,4},{6,2},{7,3},{8,9},{9,8},{10,14... | collective-permute-start | bytes 2211848 | tf_op jit(solution)/shard_map/ppermute | solution.py:49
  82.1 21.1 %collective-permute-start.16 = (bf16[4,48,1920]{2,1,0:T(8,128)(2,1)}, bf16[4,48,1920]{2,1,0:T(8,128)(2,1)}, u32[]{:S(2)}, u32[]{:S(2)}) collective-permute-start(bf16[4,48,1920]{2,1,0:T(8,128)(2,1)} %collective-permute-done.9.refs_1_), channel_id=1, source_target_pairs={{0,4},{1,5},{2,3},{3,2},{4,0},{5,1},{6,7},{7,6},{8,12},{9,13},{10,... | collective-permute-start | bytes 2211848 | tf_op jit(solution)/shard_map/ppermute | solution.py:49
  115.4 23.4 %collective-permute-start.25 = (bf16[4,48,1536]{2,1,0:T(8,128)(2,1)}, bf16[4,48,1536]{2,1,0:T(8,128)(2,1)S(1)}, u32[]{:S(2)}, u32[]{:S(2)}) collective-permute-start(bf16[4,48,1536]{2,1,0:T(8,128)(2,1)} %pad_maximum_fusion.1.refs_0_.refs_8_), channel_id=1, source_target_pairs={{0,4},{1,5},{2,3},{3,2},{4,0},{5,1},{6,7},{7,6},{8,12},{9,13},{10,... | collective-permute-start | bytes 1769480 | tf_op jit(solution)/shard_map/ppermute | solution.py:49
  117.1 21.8 %collective-permute-start.26 = (bf16[4,48,1536]{2,1,0:T(8,128)(2,1)}, bf16[4,48,1536]{2,1,0:T(8,128)(2,1)}, u32[]{:S(2)}, u32[]{:S(2)}) collective-permute-start(bf16[4,48,1536]{2,1,0:T(8,128)(2,1)} %collective-permute-done.20.refs_1_.refs_9_), channel_id=1, source_target_pairs={{0,4},{1,5},{2,3},{3,2},{4,0},{5,1},{6,7},{7,6},{8,12},{9,13},{10,... | collective-permute-start | bytes 1769480 | tf_op jit(solution)/shard_map/ppermute | solution.py:49
  118.6 23.4 %collective-permute-start.27 = (bf16[4,48,1536]{2,1,0:T(8,128)(2,1)}, bf16[4,48,1536]{2,1,0:T(8,128)(2,1)}, u32[]{:S(2)}, u32[]{:S(2)}) collective-permute-start(bf16[4,48,1536]{2,1,0:T(8,128)(2,1)} %pad_maximum_fusion.1.refs_0_.refs_8_), channel_id=1, source_target_pairs={{0,2},{1,3},{2,0},{3,1},{4,6},{5,7},{6,4},{7,5},{8,10},{9,11},{10,... | collective-permute-start | bytes 1769480 | tf_op jit(solution)/shard_map/ppermute | solution.py:49
  118.7 23.4 %collective-permute-start.28 = (bf16[4,48,1536]{2,1,0:T(8,128)(2,1)}, bf16[4,48,1536]{2,1,0:T(8,128)(2,1)}, u32[]{:S(2)}, u32[]{:S(2)}) collective-permute-start(bf16[4,48,1536]{2,1,0:T(8,128)(2,1)} %collective-permute-done.20.refs_1_.refs_9_), channel_id=1, source_target_pairs={{0,2},{1,3},{2,0},{3,1},{4,6},{5,7},{6,4},{7,5},{8,10},{9,11},{10,... | collective-permute-start | bytes 1769480 | tf_op jit(solution)/shard_map/ppermute | solution.py:49
  166.8 60.7 %collective-permute-start.31 = (bf16[1024,768]{1,0:T(8,128)(2,1)}, bf16[1024,768]{1,0:T(8,128)(2,1)}, u32[]{:S(2)}, u32[]{:S(2)}) collective-permute-start(bf16[1024,768]{1,0:T(8,128)(2,1)} %get-tuple-element.99), channel_id=1, source_target_pairs={{0,1},{1,0},{2,3},{3,2},{4,5},{5,4},{6,7},{7,6},{8,9},{9,8},{10,11... | collective-permute-start | bytes 4718600 | tf_op jit(solution)/shard_map/ppermute | solution.py:53
  220.0 45.1 %collective-permute-start.33 = (bf16[2,2,4,48,2048]{4,3,2,1,0:T(8,128)(2,1)}, bf16[2,2,4,48,2048]{4,3,2,1,0:T(8,128)(2,1)}, u32[]{:S(2)}, u32[]{:S(2)}) collective-permute-start(bf16[2,2,4,48,2048]{4,3,2,1,0:T(8,128)(2,1)} %get-tuple-element.111), channel_id=1, source_target_pairs={{0,2},{1,3},{2,0},{3,1},{4,6},{5,7},{6,4},{7,5},{8,10},{9,11},{10,... | collective-permute-start | bytes 9437192 | tf_op jit(solution)/shard_map/ppermute | solution.py:49
  243.3 21.7 %collective-permute-start.35 = (bf16[4,48,1536]{2,1,0:T(8,128)(2,1)}, bf16[4,48,1536]{2,1,0:T(8,128)(2,1)S(1)}, u32[]{:S(2)}, u32[]{:S(2)}) collective-permute-start(bf16[4,48,1536]{2,1,0:T(8,128)(2,1)} %get-tuple-element.161), channel_id=1, source_target_pairs={{0,1},{1,0},{2,6},{3,7},{4,5},{5,4},{6,2},{7,3},{8,9},{9,8},{10,14... | collective-permute-start | bytes 1769480 | tf_op jit(solution)/shard_map/ppermute | solution.py:49
  265.0 29.8 %collective-permute-start.36 = (bf16[2,4,1,48,1280]{4,3,2,1,0:T(8,128)(2,1)}, bf16[2,4,1,48,1280]{4,3,2,1,0:T(8,128)(2,1)}, u32[]{:S(2)}, u32[]{:S(2)}) collective-permute-start(bf16[2,4,1,48,1280]{4,3,2,1,0:T(8,128)(2,1)} %get-tuple-element.125), channel_id=1, source_target_pairs={{0,2},{1,3},{2,0},{3,1},{4,6},{5,7},{6,4},{7,5},{8,10},{9,11},{10,... | collective-permute-start | bytes 2949128 | tf_op jit(solution)/shard_map/ppermute | solution.py:49
  271.4 23.3 %collective-permute-start.37 = (bf16[2,4,48,2048]{3,2,1,0:T(8,128)(2,1)}, bf16[2,4,48,2048]{3,2,1,0:T(8,128)(2,1)}, u32[]{:S(2)}, u32[]{:S(2)}) collective-permute-start(bf16[2,4,48,2048]{3,2,1,0:T(8,128)(2,1)} %get-tuple-element.153), channel_id=1, source_target_pairs={{0,4},{1,5},{2,3},{3,2},{4,0},{5,1},{6,7},{7,6},{8,12},{9,13},{10,... | collective-permute-start | bytes 4718600 | tf_op jit(solution)/shard_map/ppermute | solution.py:49
  277.8 41.7 %collective-permute-start.53 = (bf16[48,1536]{1,0:T(8,128)(2,1)}, bf16[48,1536]{1,0:T(8,128)(2,1)S(1)}, u32[]{:S(2)}, u32[]{:S(2)}) collective-permute-start(bf16[48,1536]{1,0:T(8,128)(2,1)} %get-tuple-element.173), channel_id=1, source_target_pairs={{0,8},{1,9},{2,10},{3,11},{4,12},{5,13},{6,14},{7,15},{8,16},{9,17... | collective-permute-start | bytes 442376 | tf_op jit(solution)/shard_map/ppermute | solution.py:49
  277.8 43.0 %collective-permute-start.54 = (bf16[48,1536]{1,0:T(8,128)(2,1)}, bf16[48,1536]{1,0:T(8,128)(2,1)S(1)}, u32[]{:S(2)}, u32[]{:S(2)}) collective-permute-start(bf16[48,1536]{1,0:T(8,128)(2,1)} %get-tuple-element.175), channel_id=1, source_target_pairs={{0,16},{1,17},{2,18},{3,19},{4,20},{5,21},{6,22},{7,23},{8,24},{9,... | collective-permute-start | bytes 442376 | tf_op jit(solution)/shard_map/ppermute | solution.py:49
  281.0 40.4 %collective-permute-start.55 = (bf16[48,1536]{1,0:T(8,128)(2,1)S(1)}, bf16[48,1536]{1,0:T(8,128)(2,1)S(1)}, u32[]{:S(2)}, u32[]{:S(2)}) collective-permute-start(bf16[48,1536]{1,0:T(8,128)(2,1)S(1)} %get-tuple-element.174), channel_id=1, source_target_pairs={{0,24},{1,25},{2,26},{3,27},{4,28},{5,29},{6,30},{7,31},{8,0},{9,1... | collective-permute-start | bytes 442376 | tf_op jit(solution)/shard_map/ppermute | solution.py:49
  298.2 36.4 %collective-permute-start.49 = (bf16[4,48,2048]{2,1,0:T(8,128)(2,1)}, bf16[4,48,2048]{2,1,0:T(8,128)(2,1)}, u32[]{:S(2)}, u32[]{:S(2)}) collective-permute-start(bf16[4,48,2048]{2,1,0:T(8,128)(2,1)} %get-tuple-element.157), channel_id=1, source_target_pairs={{0,1},{1,0},{2,6},{3,7},{4,5},{5,4},{6,2},{7,3},{8,9},{9,8},{10,14... | collective-permute-start | bytes 2359304 | tf_op jit(solution)/shard_map/ppermute | solution.py:49
  317.4 22.5 %collective-permute-start.39 = (bf16[2,4,1,48,1280]{4,3,2,1,0:T(8,128)(2,1)}, bf16[2,4,1,48,1280]{4,3,2,1,0:T(8,128)(2,1)S(1)}, u32[]{:S(2)}, u32[]{:S(2)}) collective-permute-start(bf16[2,4,1,48,1280]{4,3,2,1,0:T(8,128)(2,1)} %get-tuple-element.133), channel_id=1, source_target_pairs={{0,2},{1,3},{2,0},{3,1},{4,6},{5,7},{6,4},{7,5},{8,10},{9,11},{10,... | collective-permute-start | bytes 2949128 | tf_op jit(solution)/shard_map/ppermute | solution.py:49
  327.6 47.3 %collective-permute-start.38 = (bf16[1024,768]{1,0:T(8,128)(2,1)}, bf16[1024,768]{1,0:T(8,128)(2,1)}, u32[]{:S(2)}, u32[]{:S(2)}) collective-permute-start(bf16[1024,768]{1,0:T(8,128)(2,1)} %get-tuple-element.129), channel_id=1, source_target_pairs={{0,1},{1,0},{2,3},{3,2},{4,5},{5,4},{6,7},{7,6},{8,9},{9,8},{10,11... | collective-permute-start | bytes 4718600 | tf_op jit(solution)/shard_map/ppermute | solution.py:53
  332.9 45.4 %collective-permute-start.48 = (bf16[1,48,1280]{2,1,0:T(8,128)(2,1)S(1)}, bf16[1,48,1280]{2,1,0:T(8,128)(2,1)S(1)}, u32[]{:S(2)}, u32[]{:S(2)}) collective-permute-start(bf16[1,48,1280]{2,1,0:T(8,128)(2,1)S(1)} %fusion.34), channel_id=1, source_target_pairs={{0,1},{1,0},{2,3},{3,2},{4,5},{5,4},{6,7},{7,6},{8,9},{9,8},{10,11... | collective-permute-start | bytes 368648 | tf_op jit(solution)/shard_map/ppermute | solution.py:49
  (60 other events, 698.9 us)
